TPU v7x, 32 devices: a whole 2x2x4 slice. The times are simulated.
32 devices in a mesh: groups: 2 (over x), ctx: 16 (over z, y, core).
Axes of the slice: x: 2, y: 2, z: 4, core: 2. Of those that a mesh axis runs over, the one named last changes fastest.
Arguments:
- pool_keys: bfloat16 [4096, 1024], P(('groups', 'ctx')), parts along dimension 0, may hold values from -6 to 6
- pool_values: bfloat16 [4096, 1024], P(('groups', 'ctx')), parts along dimension 0, may hold values from -6 to 6
- key_scales: float32 [256, 8], P(('groups', 'ctx')), parts along dimension 0, may hold values from 0.25 to 2
- value_scales: float32 [256, 8], P(('groups', 'ctx')), parts along dimension 0, may hold values from 0.25 to 2
- page_source: int32 [256], P('groups'), parts along dimension 0, may hold values from 0 to 127, as said below
- page_lengths: int32 [256], P('groups'), parts along dimension 0, may hold values from 10 to 16
- page_offsets: int32 [256], P('groups'), parts along dimension 0, may hold values from 0 to 1899, as said below
- query_positions: int32 [256], P('groups'), parts along dimension 0, may hold values from 0 to 2047
- queries: bfloat16 [256, 16384], P('groups', 'ctx'), parts along dimension 0, may hold values from -64 to 64
- out_weight: bfloat16 [16384, 16384], P('ctx'), may hold values from -0.046875 to 0.046875
Outputs:
- new_keys: bfloat16 [4096, 1024], P(('groups', 'ctx')), parts along dimension 0
- new_values: bfloat16 [4096, 1024], P(('groups', 'ctx')), parts along dimension 0
- output: bfloat16 [256, 16384], P('groups', 'ctx'), parts along dimension 0
There are 2 independent parts, one for each index of `groups`. A program takes and returns all parts, laid end to end along the dimension named above; an argument that names none is the same for every part. Nothing has to cross between parts.
Inputs may be any that keep to these rules, and one draw needn't show every extreme that they name: `page_source`: a permutation of the pool pages; the 8 pages of one device's part of the new context come from 8 different devices, and the 8 pool pages of one device go to 8 different devices. page_offsets[0] is 0, and page_offsets[c + 1] - page_offsets[c] is page_lengths[c] plus 0 to 4.
All inputs are finite; a program needn't handle non-finite values.
Results may differ from a plain program's by a relative error of at most 0.012.
The roundings to bfloat16 on the way count: a program that leaves them out, or rounds other values in their place, can miss the bound.
Values may be sent and summed in bfloat16 or wider, within the bound.
No kernel may reach another device: no remote copies, remote signals or barrier semaphores. Data moves between devices by JAX's collectives and lax.ppermute only.
A program may use at most 128 MiB of HBM per device.

v0:
```python
import math

import jax
import jax.numpy as jnp
from jax import lax
from jax.sharding import PartitionSpec as P

H = 128
KV = 8
HD = 128
PAGE = 16


rope_theta = 500000.0
scale_factor = 8.0
low_factor = 1.0
high_factor = 4.0
old_context = 8192.0
masked_score = -1e30


def inverse_freq():
    exponent = jnp.arange(0, HD, 2).astype(jnp.float32) / HD
    base_freq = 1.0 / rope_theta**exponent
    wavelength = 2.0 * math.pi / base_freq
    smooth = (old_context / wavelength - low_factor) / (high_factor - low_factor)
    blended = (1.0 - smooth) * base_freq / scale_factor + smooth * base_freq
    short_wave = wavelength < old_context / high_factor
    longer = wavelength > old_context / low_factor
    return jnp.where(short_wave, base_freq, jnp.where(longer, base_freq / scale_factor, blended))


def rotate(values, positions):
    angle = positions.astype(jnp.float32)[:, None] * inverse_freq()[None, :]
    cosine = jnp.cos(angle)[:, None, :]
    sine_part = jnp.sin(angle)[:, None, :]
    half_size = values.shape[-1] // 2
    first_half = values[..., :half_size]
    second = values[..., half_size:]
    return jnp.concatenate(
        [first_half * cosine - second * sine_part, second * cosine + first_half * sine_part],
        axis=-1,
    )


def body(
    pool_keys,
    pool_values,
    key_scales,
    value_scales,
    page_source,
    page_lengths,
    page_offsets,
    query_positions,
    queries,
    out_weight,
):
    devices = lax.axis_size("ctx")
    here_index = lax.axis_index("ctx")
    slot_count = key_scales.shape[0]
    page_count = page_source.shape[0]
    query_count = queries.shape[0]
    local_heads = queries.shape[1] // HD
    per_group = H // KV
    in_page = jnp.arange(PAGE, dtype=jnp.int32)
    inverse = (
        jnp.zeros((page_count,), jnp.int32)
        .at[page_source]
        .set(jnp.arange(page_count, dtype=jnp.int32))
    )
    held_pages = lax.dynamic_slice_in_dim(inverse, here_index * slot_count, slot_count)
    held_live = in_page[None, :] < page_lengths[held_pages][:, None]
    live_float = held_live.reshape(-1).astype(jnp.float32)[:, None, None]
    scaled_keys = (
        pool_keys.reshape(slot_count, PAGE, KV, HD).astype(jnp.float32)
        * key_scales[:, None, :, None]
    )
    scaled_values = (
        pool_values.reshape(slot_count, PAGE, KV, HD).astype(jnp.float32)
        * value_scales[:, None, :, None]
    )
    turned = rotate(
        scaled_keys.reshape(slot_count * PAGE, KV, HD), jnp.repeat(page_offsets[held_pages], PAGE)
    )
    slot_keys = (turned * live_float).astype(jnp.bfloat16).reshape(slot_count, PAGE * KV * HD)
    slot_values = (
        (scaled_values.reshape(slot_count * PAGE, KV, HD) * live_float)
        .astype(jnp.bfloat16)
        .reshape(slot_count, PAGE * KV * HD)
    )
    owner_device = held_pages // slot_count
    routing = (owner_device[None, :] == jnp.arange(devices, dtype=jnp.int32)[:, None]).astype(
        jnp.bfloat16
    )
    outgoing_keys = jnp.dot(routing, slot_keys, preferred_element_type=jnp.float32).astype(
        jnp.bfloat16
    )
    outgoing_values = jnp.dot(routing, slot_values, preferred_element_type=jnp.float32).astype(
        jnp.bfloat16
    )
    arrived_keys, arrived_values = (
        lax.all_to_all(outgoing_keys, "ctx", split_axis=0, concat_axis=0, tiled=True),
        lax.all_to_all(outgoing_values, "ctx", split_axis=0, concat_axis=0, tiled=True),
    )
    assembled_pages = here_index * slot_count + jnp.arange(slot_count, dtype=jnp.int32)
    sender = page_source[assembled_pages] // slot_count
    new_keys = arrived_keys[sender].reshape(slot_count * PAGE, KV * HD)
    new_values = arrived_values[sender].reshape(slot_count * PAGE, KV * HD)
    local_keys = slot_keys.reshape(slot_count * PAGE, KV * HD)
    local_values = slot_values.reshape(slot_count * PAGE, KV * HD)
    local_tokens = local_keys.shape[0]
    turned_q = rotate(
        queries.astype(jnp.float32).reshape(query_count, local_heads, HD), query_positions
    )
    own_queries = turned_q.astype(jnp.bfloat16).transpose(1, 0, 2)
    target = jnp.arange(devices, dtype=jnp.int32) * local_heads // per_group
    keys_by_head = local_keys.reshape(local_tokens, KV, HD).transpose(1, 0, 2)
    values_by_head = local_values.reshape(local_tokens, KV, HD).transpose(1, 0, 2)
    head_keys, head_values = (
        lax.all_to_all(keys_by_head[target], "ctx", split_axis=0, concat_axis=0, tiled=True),
        lax.all_to_all(values_by_head[target], "ctx", split_axis=0, concat_axis=0, tiled=True),
    )
    key_positions = (page_offsets[inverse][:, None] + in_page[None, :]).reshape(-1)
    key_live = (in_page[None, :] < page_lengths[inverse][:, None]).reshape(-1)
    key_positions, key_live = (key_positions, key_live)
    allowed = (key_positions[None, :] <= query_positions[:, None]) & key_live[None, :]
    span_devices = max(1, min(devices, 4096 // local_tokens))
    while span_devices > 1 and devices % span_devices:
        span_devices -= 1
    block_count = devices // span_devices
    key_blocks = head_keys.reshape(block_count, span_devices * local_tokens, HD)
    value_blocks = head_values.reshape(block_count, span_devices * local_tokens, HD)
    allowed_blocks = allowed.reshape(
        query_count, block_count, span_devices * local_tokens
    ).transpose(1, 0, 2)

    def block_scores(key_block, allow_block):
        scores = jnp.einsum(
            "hqd,kd->hqk", own_queries, key_block, preferred_element_type=jnp.float32
        ) * HD ** (-0.5)
        return jnp.where(allow_block[None], scores, masked_score)

    block_max = lax.map(
        lambda operands: jnp.max(block_scores(operands[0], operands[1]), axis=-1),
        (key_blocks, allowed_blocks),
    )
    row_max = jnp.max(block_max, axis=0)

    def weigh_block(operands):
        key_block, value_block, allow_block = operands
        weights = jnp.exp(block_scores(key_block, allow_block) - row_max[..., None])
        denominator = jnp.sum(weights, axis=-1)
        summed = jnp.einsum(
            "hqk,kd->hqd",
            weights.astype(jnp.bfloat16),
            value_block,
            preferred_element_type=jnp.float32,
        )
        return (summed, denominator)

    summed, denominator = lax.map(weigh_block, (key_blocks, value_blocks, allowed_blocks))
    summed = jnp.sum(summed, axis=0)
    denominator = jnp.sum(denominator, axis=0)
    attended = (summed / denominator[..., None]).astype(jnp.bfloat16)
    mixed = attended.transpose(1, 0, 2).reshape(query_count, local_heads * HD)
    reduced = lax.psum_scatter(
        lax.dot_general(
            out_weight, mixed, (((0,), (1,)), ((), ())), preferred_element_type=jnp.float32
        ),
        "ctx",
        scatter_dimension=0,
        tiled=True,
    )
    output = reduced.T.astype(jnp.bfloat16)
    return (new_keys, new_values, output)


def solution(mesh):
    in_specs = (
        P(("groups", "ctx"), None),
        P(("groups", "ctx"), None),
        P(("groups", "ctx"), None),
        P(("groups", "ctx"), None),
        P("groups"),
        P("groups"),
        P("groups"),
        P("groups"),
        P("groups", "ctx"),
        P("ctx", None),
    )
    out_specs = (P(("groups", "ctx"), None), P(("groups", "ctx"), None), P("groups", "ctx"))
    return jax.shard_map(body, mesh=mesh, in_specs=in_specs, out_specs=out_specs, check_vma=False)
```

profile of v0, /device:TPU:0, one launch (start us, length us, event | category | flops | bytes accessed | tf_op | source)
XLA Modules:
  0.0 205.8 jit_solution(7012284958098721424)
XLA Ops:
  8.6 1.0 scatter_custom_fusion
  10.3 1.3 gather_fusion
  12.0 0.8 copy.50
  12.7 0.8 copy.57
  13.8 1.1 copy.55
  14.9 1.1 copy.49
  17.9 1.4 gather_fusion.7
  19.3 7.4 %all-to-all-start.2 = ((bf16[16,128,128]{2,1,0:T(8,128)(2,1)}), bf16[16,128,128]{2,1,0:T(8,128)(2,1)S(1)}, u32[]{:S(2)}, u32[]{:S(2)}) async-start(bf16[16,128,128]{2,1,0:T(8,128)(2,1)} %gather_fusion.7), calls=%async_computation.2 | async-start | bytes 1048576 | tf_op jit(solution)/shard_map/all_to_all | solution.py:120
  26.7 1.2 gather_fusion.6
  28.0 1.2 gather_fusion.5
  30.2 1.4 gather_fusion.8
  32.1 8.9 %all-to-all-done.2 = bf16[16,128,128]{2,1,0:T(8,128)(2,1)S(1)} async-done(((bf16[16,128,128]{2,1,0:T(8,128)(2,1)}), bf16[16,128,128]{2,1,0:T(8,128)(2,1)S(1)}, u32[]{:S(2)}, u32[]{:S(2)}) %all-to-all-start.2) | async-done | bytes 524320 | tf_op jit(solution)/shard_map/all_to_all | solution.py:120
  41.0 4.2 %all-to-all-start.3 = ((bf16[16,128,128]{2,1,0:T(8,128)(2,1)}), bf16[16,128,128]{2,1,0:T(8,128)(2,1)S(1)}, u32[]{:S(2)}, u32[]{:S(2)}) async-start(bf16[16,128,128]{2,1,0:T(8,128)(2,1)} %gather_fusion.8), calls=%async_computation.3 | async-start | bytes 1048576 | tf_op jit(solution)/shard_map/all_to_all | solution.py:121
  45.4 1.7 fusion.2
  47.1 3.2 %copy-done.4 = f32[8,128,2048]{2,1,0:T(8,128)} copy-done((f32[8,128,2048]{2,1,0:T(8,128)}, f32[8,128,2048]{2,1,0:T(8,128)S(1)}, u32[]{:S(2)}) %copy-start.4) | copy-done | bytes 8388632
  50.4 2.2 %fusion.3 = f32[8,128]{1,0:T(8,128)S(1)} fusion(f32[8,128,2048]{2,1,0:T(8,128)S(1)} %get-tuple-element.60, f32[8,128]{1,0:T(8,128)S(1)} %get-tuple-element.59, pred[128,2048]{1,0:T(8,128)(4,1)S(1)} %compare_and_fusion), kind=kLoop, calls=%fused_computation.18 | loop fusion | flops 8387584 | bytes 8658944 | tf_op jit(solution)/shard_map/while/body/eval_jaxpr/reduce_sum | solution.py:152
  52.6 6.8 %all-to-all-done.3 = bf16[16,128,128]{2,1,0:T(8,128)(2,1)S(1)} async-done(((bf16[16,128,128]{2,1,0:T(8,128)(2,1)}), bf16[16,128,128]{2,1,0:T(8,128)(2,1)S(1)}, u32[]{:S(2)}, u32[]{:S(2)}) %all-to-all-start.3) | async-done | bytes 524320 | tf_op jit(solution)/shard_map/all_to_all | solution.py:121
  59.4 5.5 %fusion.14 = bf16[128,8,128]{0,2,1:T(8,128)(2,1)S(1)} fusion(bf16[2048,128,1]{1,0,2:T(8,128)(2,1)S(1)} %bitcast.74, f32[8,128,2048]{2,1,0:T(8,128)} %copy-done.4, f32[8,128]{1,0:T(8,128)S(1)} %get-tuple-element.59, pred[128,2048]{1,0:T(8,128)(4,1)S(1)} %compare_and_fusion, f32[128,8]{0,1:T(8,128)S(1)} %bitcast.76), kind=kOutput, calls=%fused_computation.25 | convolution fusion | flops 545521664 | bytes 9445376 | tf_op jit(solution)/shard_map/while/body/eval_jaxpr/hqk,kd->hqd/dot_general | solution.py:153
  64.9 18.6 %convolution_bitcast_fusion = f32[16384,128]{0,1:T(8,128)} fusion(bf16[128,1024]{0,1:T(8,128)(2,1)S(1)} %bitcast.75, bf16[1024,16384]{1,0:T(8,128)(2,1)} %param.19), kind=kOutput, calls=%fused_computation.10 | convolution fusion | flops 4294967296 | bytes 42205184 | tf_op jit(solution)/shard_map/dot_general | solution.py:167
  85.3 1.0 reduce.1
  86.3 1.2 reshape.473
  87.5 4.2 %all-to-all-start.1 = ((bf16[16,2,8192]{2,1,0:T(2,128)(2,1)}), bf16[16,2,8192]{2,1,0:T(2,128)(2,1)S(1)}, u32[]{:S(2)}, u32[]{:S(2)}) async-start(bf16[16,2,8192]{2,1,0:T(2,128)(2,1)} %reshape.473), calls=%async_computation.1 | async-start | bytes 1048576 | tf_op jit(solution)/shard_map/all_to_all | solution.py:103
  92.4 1.0 reduce
  93.5 1.2 reshape.471
  94.7 11.3 %all-to-all-done.1 = bf16[16,2,8192]{2,1,0:T(2,128)(2,1)S(1)} async-done(((bf16[16,2,8192]{2,1,0:T(2,128)(2,1)}), bf16[16,2,8192]{2,1,0:T(2,128)(2,1)S(1)}, u32[]{:S(2)}, u32[]{:S(2)}) %all-to-all-start.1) | async-done | bytes 524320 | tf_op jit(solution)/shard_map/all_to_all | solution.py:103
  106.0 4.2 %all-to-all-start = ((bf16[16,2,8192]{2,1,0:T(2,128)(2,1)}), bf16[16,2,8192]{2,1,0:T(2,128)(2,1)S(1)}, u32[]{:S(2)}, u32[]{:S(2)}) async-start(bf16[16,2,8192]{2,1,0:T(2,128)(2,1)} %reshape.471), calls=%async_computation | async-start | bytes 1048576 | tf_op jit(solution)/shard_map/all_to_all | solution.py:102
  112.0 0.7 gather_fusion.4
  112.7 0.8 reshape.372
  113.5 16.4 %all-to-all-done = bf16[16,2,8192]{2,1,0:T(2,128)(2,1)S(1)} async-done(((bf16[16,2,8192]{2,1,0:T(2,128)(2,1)}), bf16[16,2,8192]{2,1,0:T(2,128)(2,1)S(1)}, u32[]{:S(2)}, u32[]{:S(2)}) %all-to-all-start) | async-done | bytes 524320 | tf_op jit(solution)/shard_map/all_to_all | solution.py:102
  131.8 0.8 reshape.371
  132.6 64.6 %reduce-scatter.2.cloned.1.call-done = f32[1024,128]{0,1:T(8,128)} async-done(((f32[16384,128]{0,1:T(8,128)}), f32[1024,128]{0,1:T(8,128)}) %reduce-scatter.2.cloned.1.call-update) | async-done | bytes 524304 | tf_op jit(solution)/shard_map/reduce_scatter | solution.py:166
  197.1 1.8 convert_bitcast_fusion
  (74 shorter events, 12.2 us)
Async XLA Ops:
  7.2 2.5 %copy-start = (s32[128]{0:T(128)S(1)}, s32[128]{0:T(128)}, u32[]{:S(2)}) copy-start(s32[128]{0:T(128)} %param.15) | copy-start | bytes 1540
  7.2 20.8 %copy-start.2 = (s32[128]{0:T(128)S(1)}, s32[128]{0:T(128)}, u32[]{:S(2)}) copy-start(s32[128]{0:T(128)} %param.16) | copy-start | bytes 1540
  7.2 22.4 %copy-start.5 = (bf16[128,1024]{1,0:T(8,128)(2,1)S(1)}, bf16[128,1024]{1,0:T(8,128)(2,1)}, u32[]{:S(2)}) copy-start(bf16[128,1024]{1,0:T(8,128)(2,1)} %param.18) | copy-start | bytes 786436
  16.3 15.6 %copy-start.6 = (s32[128]{0:T(128)S(1)}, s32[128]{0:T(128)}, u32[]{:S(2)}) copy-start(s32[128]{0:T(128)} %param.17) | copy-start | bytes 1540
  19.3 21.7 %all-to-all-start.2 = ((bf16[16,128,128]{2,1,0:T(8,128)(2,1)}), bf16[16,128,128]{2,1,0:T(8,128)(2,1)S(1)}, u32[]{:S(2)}, u32[]{:S(2)}) async-start(bf16[16,128,128]{2,1,0:T(8,128)(2,1)} %gather_fusion.7), calls=%async_computation.2 | async-start | bytes 1048576 | tf_op jit(solution)/shard_map/all_to_all | solution.py:120
  41.0 18.4 %all-to-all-start.3 = ((bf16[16,128,128]{2,1,0:T(8,128)(2,1)}), bf16[16,128,128]{2,1,0:T(8,128)(2,1)S(1)}, u32[]{:S(2)}, u32[]{:S(2)}) async-start(bf16[16,128,128]{2,1,0:T(8,128)(2,1)} %gather_fusion.8), calls=%async_computation.3 | async-start | bytes 1048576 | tf_op jit(solution)/shard_map/all_to_all | solution.py:121
  45.2 152.0 %reduce-scatter.2.cloned.1.call-start = ((), (), s32[]{:S(2)}) async-start(), calls=%async_computation.5 | async-start | bytes 8912896 | tf_op jit(solution)/shard_map/reduce_scatter | solution.py:166
  47.1 3.2 %copy-start.4 = (f32[8,128,2048]{2,1,0:T(8,128)}, f32[8,128,2048]{2,1,0:T(8,128)S(1)}, u32[]{:S(2)}) copy-start(f32[8,128,2048]{2,1,0:T(8,128)S(1)} %get-tuple-element.60) | copy-start | bytes 25165828
  83.6 26.5 %copy-start.3 = (s32[128]{0:T(128)S(1)}, s32[128]{0:T(128)}, u32[]{:S(2)}) copy-start(s32[128]{0:T(128)} %param.14) | copy-start | bytes 1540
  87.5 18.4 %all-to-all-start.1 = ((bf16[16,2,8192]{2,1,0:T(2,128)(2,1)}), bf16[16,2,8192]{2,1,0:T(2,128)(2,1)S(1)}, u32[]{:S(2)}, u32[]{:S(2)}) async-start(bf16[16,2,8192]{2,1,0:T(2,128)(2,1)} %reshape.473), calls=%async_computation.1 | async-start | bytes 1048576 | tf_op jit(solution)/shard_map/all_to_all | solution.py:103
  92.1 106.8 %copy-start.1 = (s32[128]{0:T(128)S(1)}, s32[128]{0:T(128)}, u32[]{:S(2)}) copy-start(s32[128]{0:T(128)} %param.15) | copy-start | bytes 1540
  106.0 24.0 %all-to-all-start = ((bf16[16,2,8192]{2,1,0:T(2,128)(2,1)}), bf16[16,2,8192]{2,1,0:T(2,128)(2,1)S(1)}, u32[]{:S(2)}, u32[]{:S(2)}) async-start(bf16[16,2,8192]{2,1,0:T(2,128)(2,1)} %reshape.471), calls=%async_computation | async-start | bytes 1048576 | tf_op jit(solution)/shard_map/all_to_all | solution.py:102
Sparse Core Ops, SparseCore 0:
  83.7 113.4 reduce-scatter.1
where the time goes:
time: 207 us; the launch traced here: 206 us
  waiting for transfers between devices  108 us (52%)
  local copies, waits for them, and re-layouts  27.2 us (13%)
  matrix products  26.4 us (13%)
  starting transfers between devices  20.1 us (10%)
  between operations  14.5 us (7%)
  other arithmetic  9.61 us (5%)
    reduce_scatter x1, waiting for transfers between devices, body(): lax.psum_scatter(lax.dot_general(out_weight, mixed, (((0,), (1,)), ((), (...  64.6 us
    dot_general x1, matrix products, body(): lax.dot_general(out_weight, mixed, (((0,), (1,)), ((), ())), preferred_el...  18.6 us
    all_to_all x1, waiting for transfers between devices, body(): lax.all_to_all(outgoing_keys, 'ctx', split_axis=0, concat_axis=0, tiled=T...  16.4 us
    unnamed x28, local copies, waits for them, and re-layouts  12.3 us
    all_to_all x1, waiting for transfers between devices, body(): lax.all_to_all(outgoing_values, 'ctx', split_axis=0, concat_axis=0, tiled...  11.3 us
    all_to_all x1, waiting for transfers between devices, body(): lax.all_to_all(keys_by_head[target], 'ctx', split_axis=0, concat_axis=0,...  8.89 us
    all_to_all x1, starting transfers between devices, body(): lax.all_to_all(keys_by_head[target], 'ctx', split_axis=0, concat_axis=0,...  7.41 us
    all_to_all x1, waiting for transfers between devices, body(): lax.all_to_all(values_by_head[target], 'ctx', split_axis=0, concat_axis=0...  6.83 us
  transfers between devices with their start and end apart: 5, of which 5 were waited for; matrix products, arithmetic and copies ran while one was open for 11% of the time, Pallas kernels for 0%

commit v1 on v0

--- a/solution.py
+++ b/solution.py
@@ -2,13 +2,18 @@
 
 import jax
 import jax.numpy as jnp
+import numpy as np
 from jax import lax
+from jax.experimental import pallas as pl
+from jax.experimental.pallas import tpu as pltpu
 from jax.sharding import PartitionSpec as P
+
 
 H = 128
 KV = 8
 HD = 128
 PAGE = 16
+MIB = 1 << 20
 
 
 rope_theta = 500000.0
@@ -17,9 +22,509 @@
 high_factor = 4.0
 old_context = 8192.0
 masked_score = -1e30
+far_position = 1e9
+VMEM = pl.BlockSpec(memory_space=pltpu.VMEM)
+SMEM = pl.BlockSpec(memory_space=pltpu.SMEM)
+HBM = pl.BlockSpec(memory_space=pltpu.HBM)
+DMA = pltpu.SemaphoreType.DMA
 
 
 def inverse_freq():
+    exponent = np.arange(0, HD, 2).astype(np.float64) / HD
+    base_freq = 1.0 / rope_theta**exponent
+    wavelength = 2.0 * math.pi / base_freq
+    smooth = (old_context / wavelength - low_factor) / (high_factor - low_factor)
+    blended = (1.0 - smooth) * base_freq / scale_factor + smooth * base_freq
+    short_wave = wavelength < old_context / high_factor
+    longer = wavelength > old_context / low_factor
+    return np.where(
+        short_wave, base_freq, np.where(longer, base_freq / scale_factor, blended)
+    ).astype(np.float32)
+
+
+def lane_tables():
+    freq = inverse_freq()
+    sign = np.repeat([-1.0, 1.0], HD // 2)
+    return jnp.asarray(np.stack([np.concatenate([freq, freq]), sign]).astype(np.float32))
+
+
+def params(mib):
+    return pltpu.CompilerParams(vmem_limit_bytes=mib * MIB)
+
+
+def cost(flops, moved, exps=0):
+    return pl.CostEstimate(flops=flops, bytes_accessed=moved, transcendentals=exps)
+
+
+def shape(dims, dtype=jnp.bfloat16):
+    return jax.ShapeDtypeStruct(dims, dtype)
+
+
+def cos_sin(position, table_ref):
+    angle = position * table_ref[0:1, :]
+    return jnp.cos(angle), jnp.sin(angle) * table_ref[1:2, :]
+
+
+def turn(x, cosine, sine):
+    return x * cosine + pltpu.roll(x, HD // 2, 1) * sine
+
+
+def column(row):
+    n = row.shape[1]
+    same = lax.broadcasted_iota(jnp.int32, (n, n), 0) == lax.broadcasted_iota(jnp.int32, (n, n), 1)
+    return jnp.sum(jnp.where(same, row, 0.0), axis=1, keepdims=True)
+
+
+def fetch(pairs, sems):
+    copies = [pltpu.make_async_copy(a, b, sems.at[at]) for at, (a, b) in enumerate(pairs)]
+    for copy in copies:
+        copy.start()
+    for copy in copies:
+        copy.wait()
+
+
+def in_hbm(xs):
+    return [pltpu.with_memory_space_constraint(x, pltpu.HBM) for x in xs]
+
+
+def vmem_like(x):
+    return pltpu.VMEM(x.shape, x.dtype)
+
+
+def rows_kernel(here_ref, *refs):
+    inputs, out_refs, scratch, sems = refs[:8], refs[8:-9], refs[-9:-1], refs[-1]
+    fetch(list(zip(inputs, scratch)), sems)
+    ks_ref, vs_ref, table_ref, source_ref, lengths_ref, offsets_ref, pk_ref, pv_ref = scratch
+    rows = pk_ref.shape[0]
+    slots = rows // PAGE
+    pages = source_ref.shape[1]
+    row = lax.broadcasted_iota(jnp.int32, (rows, pages), 0)
+    match = source_ref[...] == here_ref[0] * slots + row // PAGE
+
+    def pick(ref):
+        return jnp.sum(jnp.where(match, ref[...].astype(jnp.float32), 0.0), axis=1, keepdims=True)
+
+    position, length = pick(offsets_ref), pick(lengths_ref)
+    cosine, sine = cos_sin(position, table_ref)
+    token = (lax.broadcasted_iota(jnp.int32, (rows, 1), 0) % PAGE).astype(jnp.float32)
+    live = jnp.broadcast_to((token < length).astype(jnp.float32), (rows, HD))
+    for piece, out_ref in enumerate(out_refs):
+        head = jnp.bitwise_xor(here_ref[0] // 2, piece)
+        lanes = pl.ds(pl.multiple_of(head * HD, HD), HD)
+        for slot in range(slots):
+            part = slice(slot * PAGE, (slot + 1) * PAGE)
+            k = pk_ref[part, lanes].astype(jnp.float32) * ks_ref[slot, head]
+            k = turn(k, cosine[part], sine[part]) * live[part]
+            out_ref[0, part, :] = k.astype(jnp.bfloat16)
+            v = pv_ref[part, lanes].astype(jnp.float32) * vs_ref[slot, head]
+            out_ref[1, part, :] = (v * live[part]).astype(jnp.bfloat16)
+
+
+def prepare_rows(here, pool_keys, pool_values, key_scales, value_scales, source, lengths, offsets):
+    rows = pool_keys.shape[0]
+    table = lane_tables()
+    small = [pltpu.SMEM(key_scales.shape, jnp.float32)] * 2
+    inputs = (key_scales, value_scales, table, source, lengths, offsets, pool_keys, pool_values)
+    return pl.pallas_call(
+        rows_kernel,
+        out_shape=[shape((2, rows, HD))] * KV,
+        in_specs=[SMEM] + [HBM] * 8,
+        out_specs=[VMEM] * KV,
+        scratch_shapes=small + [vmem_like(x) for x in inputs[2:]] + [DMA((8,))],
+        name="prepare_rows",
+        compiler_params=params(6),
+        cost_estimate=cost(20 * rows * KV * HD, 8 * rows * KV * HD),
+    )(here, *in_hbm(inputs))
+
+
+def side_kernel(here_ref, *refs):
+    inputs, (out_ref, kpos_ref), scratch, sems = refs[:6], refs[6:8], refs[8:14], refs[14]
+    fetch(list(zip(inputs, scratch)), sems)
+    table_ref, source_ref, lengths_ref, offsets_ref, position_ref, q_ref = scratch
+    count = q_ref.shape[0]
+    cosine, sine = cos_sin(column(position_ref[...].astype(jnp.float32)), table_ref)
+    for head in range(q_ref.shape[1] // HD):
+        q = q_ref[:, head * HD : (head + 1) * HD].astype(jnp.float32)
+        out_ref[head * count : (head + 1) * count, :] = turn(q, cosine, sine).astype(jnp.bfloat16)
+    source = column(source_ref[...].astype(jnp.float32))
+    length = column(lengths_ref[...].astype(jnp.float32))
+    offset = column(offsets_ref[...].astype(jnp.float32))
+    tokens = kpos_ref.shape[1]
+    rows = tokens // (2 * KV)
+    slots = rows // PAGE
+    at = lax.broadcasted_iota(jnp.int32, (1, rows), 1)
+    token = (at % PAGE).astype(jnp.float32)
+    where = jnp.where(token < length, offset + token, far_position)
+    for group in range(2 * KV):
+        half, piece = group // KV, group % KV
+        device = jnp.bitwise_xor(here_ref[0], 2 * piece + half)
+        page = (device * slots + at // PAGE).astype(jnp.float32)
+        kpos_ref[:, group * rows : (group + 1) * rows] = jnp.sum(
+            jnp.where(source == page, where, 0.0), axis=0, keepdims=True
+        )
+
+
+def side(here, source, lengths, offsets, positions, queries):
+    count, width = queries.shape
+    tokens = source.shape[1] * PAGE
+    inputs = (lane_tables(), source, lengths, offsets, positions, queries)
+    return pl.pallas_call(
+        side_kernel,
+        out_shape=(shape((count * (width // HD), HD)), shape((1, tokens), jnp.float32)),
+        in_specs=[SMEM] + [HBM] * 6,
+        out_specs=(VMEM, VMEM),
+        scratch_shapes=[vmem_like(x) for x in inputs] + [DMA((6,))],
+        name="side",
+        compiler_params=params(6),
+        cost_estimate=cost(8 * count * width, 64 * MIB),
+    )(here, *in_hbm(inputs))
+
+
+def assemble_kernel(*refs):
+    for at, ref in enumerate(refs[:-1]):
+        refs[-1][at] = ref[...]
+
+
+def assemble(pieces):
+    dims = (len(pieces), *pieces[0].shape)
+    return pl.pallas_call(
+        assemble_kernel,
+        out_shape=shape(dims),
+        in_specs=[VMEM] * len(pieces),
+        out_specs=VMEM,
+        compiler_params=params(2),
+        cost_estimate=cost(0, 4 * math.prod(dims)),
+    )(*pieces)
+
+
+def pages_kernel(here_ref, source_ref, *refs):
+    context, out_refs, page_ref, place_ref = refs[: -KV - 2], refs[-KV - 2 : -2], refs[-2], refs[-1]
+    pages = source_ref.shape[0]
+    slots = pages // (2 * KV)
+    here = here_ref[0]
+    kind = here % 2
+    for page in range(pages):
+        place_ref[source_ref[page]] = page
+    group = 0
+    for ref in context:
+        for at in range(ref.shape[0]):
+            half, piece = group // KV, group % KV
+            device = jnp.bitwise_xor(here, 2 * piece + half)
+            for slot in range(slots):
+                page = place_ref[device * slots + slot]
+                page_ref[page] = ref[at, kind, slot * PAGE : (slot + 1) * PAGE, :]
+            group += 1
+    for piece, out_ref in enumerate(out_refs):
+        first = jnp.bitwise_xor(here // 2, piece) * 2 * slots
+        out_ref[...] = page_ref[pl.ds(first, 2 * slots)]
+
+
+def order_pages(here, source, context):
+    pages = source.shape[0]
+    return pl.pallas_call(
+        pages_kernel,
+        out_shape=[shape((pages // KV, PAGE, HD))] * KV,
+        in_specs=[SMEM, SMEM] + [VMEM] * len(context),
+        out_specs=[VMEM] * KV,
+        scratch_shapes=[pltpu.VMEM((pages, PAGE, HD), jnp.bfloat16), pltpu.SMEM((pages,), jnp.int32)],
+        name="order_pages",
+        compiler_params=params(4),
+        cost_estimate=cost(0, 4 * pages * PAGE * HD),
+    )(here, source, *context)
+
+
+def collect_kernel(here_ref, *refs):
+    pieces, (keep_ref, send_ref) = refs[:-2], refs[-2:]
+    rows = keep_ref.shape[0]
+    slots = rows // PAGE
+    core = here_ref[0] % 2
+    for piece, ref in enumerate(pieces):
+        head = jnp.bitwise_xor(here_ref[0] // 2, piece)
+        lanes = pl.ds(pl.multiple_of(head * HD, HD), HD)
+        keep_ref[:, lanes] = ref[pl.ds(core * slots, slots)].reshape(rows, HD)
+        send_ref[:, lanes] = ref[pl.ds((1 - core) * slots, slots)].reshape(rows, HD)
+
+
+def collect_heads(here, pieces):
+    rows = pieces[0].shape[0] * PAGE // 2
+    out = shape((rows, KV * HD))
+    return pl.pallas_call(
+        collect_kernel,
+        out_shape=(out, out),
+        in_specs=[SMEM] + [VMEM] * KV,
+        out_specs=(VMEM, VMEM),
+        name="collect_heads",
+        compiler_params=params(4),
+        cost_estimate=cost(0, 8 * rows * KV * HD),
+    )(here, *pieces)
+
+
+def settle_kernel(here_ref, mine_ref, other_ref, keys_ref, values_ref):
+    first = here_ref[0] % 2 == 0
+    keys_ref[...] = jnp.where(first, mine_ref[...], other_ref[...])
+    values_ref[...] = jnp.where(first, other_ref[...], mine_ref[...])
+
+
+def settle(here, mine, other):
+    return pl.pallas_call(
+        settle_kernel,
+        out_shape=(shape(mine.shape), shape(mine.shape)),
+        in_specs=[SMEM, VMEM, VMEM],
+        out_specs=(VMEM, VMEM),
+        name="settle",
+        compiler_params=params(4),
+        cost_estimate=cost(0, 8 * math.prod(mine.shape)),
+    )(here, mine, other)
+
+
+def attention_kernel(*refs):
+    context, (q_ref, kpos_ref, qpos_ref, out_ref, s_ref) = refs[:-5], refs[-5:]
+    count = qpos_ref.shape[1]
+    heads = q_ref.shape[0] // count
+    rows = context[0].shape[2]
+    blocks, at = [], 0
+    for ref in context:
+        step = max(1, min(ref.shape[0], 512 // rows))
+        for first in range(0, ref.shape[0], step):
+            blocks.append((ref, slice(first, first + step), slice(at, at + step * rows)))
+            at += step * rows
+    block = step * rows
+    scale = HD**-0.5 * math.log2(math.e)
+    qpos = column(qpos_ref[...].astype(jnp.float32))
+
+    def one(head, carry):
+        q = q_ref[pl.ds(pl.multiple_of(head * count, count), count), :]
+        top = jnp.full((count, HD), masked_score, jnp.float32)
+        for ref, chips, lanes in blocks:
+            s = lax.dot_general(
+                q,
+                ref[chips, 0].reshape(block, HD),
+                (((1,), (1,)), ((), ())),
+                preferred_element_type=jnp.float32,
+            )
+            s = jnp.where(kpos_ref[:, lanes] <= qpos, s, masked_score)
+            s_ref[:, lanes] = s
+            for lane in range(0, block, HD):
+                top = jnp.maximum(top, s[:, lane : lane + HD])
+        top = jnp.max(top, axis=1, keepdims=True)
+        total = jnp.zeros((count, HD), jnp.float32)
+        summed = jnp.zeros((count, HD), jnp.float32)
+        for ref, chips, lanes in blocks:
+            w = jnp.exp2((s_ref[:, lanes] - top) * scale)
+            for lane in range(0, block, HD):
+                total = total + w[:, lane : lane + HD]
+            summed = summed + jnp.dot(
+                w.astype(jnp.bfloat16),
+                ref[chips, 1].reshape(block, HD),
+                preferred_element_type=jnp.float32,
+            )
+        total = jnp.sum(total, axis=1, keepdims=True)
+        out_ref[:, pl.ds(pl.multiple_of(head * HD, HD), HD)] = (summed / total).astype(jnp.bfloat16)
+        return carry
+
+    lax.fori_loop(0, heads, one, 0)
+
+
+def attend(context, q, key_positions, query_positions):
+    tokens = key_positions.shape[1]
+    count = query_positions.shape[1]
+    heads = q.shape[0] // count
+    return pl.pallas_call(
+        attention_kernel,
+        out_shape=shape((count, heads * HD)),
+        in_specs=[VMEM] * (len(context) + 3),
+        out_specs=VMEM,
+        scratch_shapes=[pltpu.VMEM((count, tokens), jnp.float32)],
+        name="attend",
+        compiler_params=params(6),
+        cost_estimate=cost(
+            4 * count * heads * tokens * HD, 4 * tokens * HD, count * heads * tokens
+        ),
+    )(*context, q, key_positions, query_positions)
+
+
+def fold_masks(bits):
+    masks = [0]
+    for bit in reversed(bits):
+        masks = masks + [m | bit for m in masks]
+    return masks
+
+
+def columns_of(here_ref, mask, width, start, w_ref):
+    own_width = w_ref.shape[1] // (2 * KV)
+    first = jnp.bitwise_xor(here_ref[0], mask) * own_width + start
+    return pl.ds(pl.multiple_of(first, HD), width)
+
+
+def project_send_kernel(masks, start, here_ref, x_ref, w_ref, out_ref):
+    for at, mask in enumerate(masks):
+        columns = columns_of(here_ref, mask, out_ref.shape[2], start, w_ref)
+        out_ref[at] = jnp.dot(
+            x_ref[...], w_ref[:, columns], preferred_element_type=jnp.float32
+        ).astype(jnp.bfloat16)
+
+
+def project_keep_kernel(masks, start, here_ref, x_ref, w_ref, got_ref, send_ref, keep_ref):
+    half = len(masks) // 2
+    for at in list(range(half, 2 * half)) + list(range(half)):
+        columns = columns_of(here_ref, masks[at], got_ref.shape[2], start, w_ref)
+        y = jnp.dot(x_ref[...], w_ref[:, columns], preferred_element_type=jnp.float32)
+        y = y + got_ref[at].astype(jnp.float32)
+        if at >= half:
+            send_ref[at - half] = y.astype(jnp.bfloat16)
+        else:
+            keep_ref[at] = y
+
+
+def project_cost(x, w, columns):
+    return cost(2 * x.shape[0] * w.shape[0] * columns, 2 * w.shape[0] * columns)
+
+
+def project_send(here, mixed, weight, masks, start, width):
+    count = mixed.shape[0]
+    return pl.pallas_call(
+        lambda *refs: project_send_kernel(masks, start, *refs),
+        out_shape=shape((len(masks), count, width)),
+        in_specs=[SMEM, VMEM, VMEM],
+        out_specs=VMEM,
+        compiler_params=params(6),
+        cost_estimate=project_cost(mixed, weight, len(masks) * width),
+    )(here, mixed, weight)
+
+
+def project_keep(here, mixed, weight, got, masks, start):
+    count = mixed.shape[0]
+    half, width = len(masks) // 2, got.shape[2]
+    return pl.pallas_call(
+        lambda *refs: project_keep_kernel(masks, start, *refs),
+        out_shape=(shape((half, count, width)), shape((half, count, width), jnp.float32)),
+        in_specs=[SMEM, VMEM, VMEM, VMEM],
+        out_specs=(VMEM, VMEM),
+        compiler_params=params(6),
+        cost_estimate=project_cost(mixed, weight, len(masks) * width),
+    )(here, mixed, weight, got)
+
+
+def fold_kernel(keep_ref, got_ref, send_ref, left_ref):
+    left = left_ref.shape[0]
+    for at in range(left):
+        send_ref[at] = (keep_ref[left + at] + got_ref[left + at].astype(jnp.float32)).astype(
+            jnp.bfloat16
+        )
+    for at in range(left):
+        left_ref[at] = keep_ref[at] + got_ref[at].astype(jnp.float32)
+
+
+def fold(keep, got):
+    owners, count, width = keep.shape
+    half = (owners // 2, count, width)
+    return pl.pallas_call(
+        fold_kernel,
+        out_shape=(shape(half), shape(half, jnp.float32)),
+        in_specs=[VMEM, VMEM],
+        out_specs=(VMEM, VMEM),
+        compiler_params=params(4),
+        cost_estimate=cost(owners * count * width, 8 * owners * count * width),
+    )(keep, got)
+
+
+def finish_kernel(*refs):
+    out_ref, at = refs[-1], 0
+    for keep_ref, got_ref in zip(refs[:-1:2], refs[1:-1:2]):
+        width = keep_ref.shape[2]
+        total = keep_ref[0] + got_ref[0].astype(jnp.float32)
+        out_ref[:, at : at + width] = total.astype(jnp.bfloat16)
+        at += width
+
+
+def finish(pairs):
+    flat = [x for pair in pairs for x in pair]
+    count = flat[0].shape[1]
+    width = sum(keep.shape[2] for keep, _ in pairs)
+    return pl.pallas_call(
+        finish_kernel,
+        out_shape=shape((count, width)),
+        in_specs=[VMEM] * len(flat),
+        out_specs=VMEM,
+        name="finish",
+        compiler_params=params(4),
+        cost_estimate=cost(count * width, 8 * count * width),
+    )(*flat)
+
+
+def swap(x, bits, devices):
+    return lax.ppermute(x, "ctx", [(d, d ^ bits) for d in range(devices)])
+
+
+def after(x, *others):
+    return lax.optimization_barrier((x, *others))[0]
+
+
+def plan(devices, own_width):
+    bits = [1 << b for b in range(devices.bit_length() - 1)]
+    half = own_width // 2
+    return [
+        (0, half, bits),
+        (half, half, [bits[0], bits[2], bits[1]] + bits[3:]),
+    ]
+
+
+def project_and_scatter(here, devices, x, weight, chunks):
+    masks = [fold_masks(order) for _, _, order in chunks]
+    half = devices // 2
+    state, got = [], []
+    for at, (start, width, order) in enumerate(chunks):
+        out = project_send(here, x, weight, masks[at][half:], start, width)
+        got.append(swap(out, order[0], devices))
+        x = after(x, out)
+    for at, (start, _, _) in enumerate(chunks):
+        send, keep = project_keep(here, x, weight, got[at], masks[at][:half], start)
+        state.append((send, keep))
+        x = after(x, send)
+    stages = len(chunks[0][2])
+    for stage in range(1, stages):
+        arrived = [swap(send, chunks[at][2][stage], devices) for at, (send, _) in enumerate(state)]
+        if stage + 1 < stages:
+            state = [fold(keep, got) for (_, keep), got in zip(state, arrived)]
+    return finish([(keep, got) for (_, keep), got in zip(state, arrived)])
+
+
+def body(
+    pool_keys,
+    pool_values,
+    key_scales,
+    value_scales,
+    page_source,
+    page_lengths,
+    page_offsets,
+    query_positions,
+    queries,
+    out_weight,
+):
+    devices = lax.axis_size("ctx")
+    here = lax.axis_index("ctx").astype(jnp.int32)[None]
+    source, lengths, offsets = page_source[None], page_lengths[None], page_offsets[None]
+    positions = query_positions[None]
+    pieces = prepare_rows(
+        here, pool_keys, pool_values, key_scales, value_scales, source, lengths, offsets
+    )
+    far = range(KV // 2, KV)
+    arrived = [pieces[0]] + [swap(pieces[k], 2 * k, devices) for k in range(1, KV)]
+    turned, key_positions = side(here, source, lengths, offsets, positions, queries)
+    chunks = plan(devices, out_weight.shape[1] // devices)
+    near = assemble(arrived[: KV // 2])
+    far = assemble(arrived[KV // 2 :])
+    context = [near, far, swap(near, 1, devices), swap(far, 1, devices)]
+    leaving = order_pages(here, page_source, context)
+    pages = [leaving[0]] + [swap(leaving[k], 2 * k, devices) for k in range(1, KV)]
+    mixed = attend(context, turned, key_positions, positions)
+    output = project_and_scatter(here, devices, mixed, out_weight, chunks)
+    mine, partner = collect_heads(here, pages)
+    new_keys, new_values = settle(here, mine, swap(partner, 1, devices))
+    return (new_keys, new_values, output)
+
+
+def wide_inverse_freq():
     exponent = jnp.arange(0, HD, 2).astype(jnp.float32) / HD
     base_freq = 1.0 / rope_theta**exponent
     wavelength = 2.0 * math.pi / base_freq
@@ -31,7 +536,7 @@
 
 
 def rotate(values, positions):
-    angle = positions.astype(jnp.float32)[:, None] * inverse_freq()[None, :]
+    angle = positions.astype(jnp.float32)[:, None] * wide_inverse_freq()[None, :]
     cosine = jnp.cos(angle)[:, None, :]
     sine_part = jnp.sin(angle)[:, None, :]
     half_size = values.shape[-1] // 2
@@ -43,7 +548,7 @@
     )
 
 
-def body(
+def wide_body(
     pool_keys,
     pool_values,
     key_scales,
@@ -189,4 +694,8 @@
         P("ctx", None),
     )
     out_specs = (P(("groups", "ctx"), None), P(("groups", "ctx"), None), P("groups", "ctx"))
-    return jax.shard_map(body, mesh=mesh, in_specs=in_specs, out_specs=out_specs, check_vma=False)
+    fits = mesh.shape["ctx"] == 2 * KV
+    chosen = body if fits else wide_body
+    return jax.shard_map(
+        chosen, mesh=mesh, in_specs=in_specs, out_specs=out_specs, check_vma=False
+    )

time: 207 us -> 94.9 us (0.46)
  waiting for transfers between devices: 108 us -> 30.8 us
  matrix products: 26.4 us -> 0 us
  Pallas kernels: 0 us -> 17.7 us
  local copies, waits for them, and re-layouts: 27.2 us -> 11.2 us
  starting transfers between devices: 20.1 us -> 34.2 us
  between operations: 14.5 us -> 0.84 us
  other arithmetic: 9.61 us -> 0 us
    reduce_scatter x1 -> x0, waiting for transfers between devices: 64.6 us -> none  [body(): lax.psum_scatter(lax.dot_general(out_weight, mixed, (((0,), (1,)), ((), (...]
    all_to_all x4 -> x0, waiting for transfers between devices: 43.4 us -> none  [the longest x1 16.4 us: body(): lax.all_to_all(outgoing_keys, 'ctx', split_axis=0, concat_axis=0, tiled=T...]
    ppermute x0 -> x25, starting transfers between devices: none -> 34.2 us  [swap(): return lax.ppermute(x, 'ctx', [(d, d ^ bits) for d in range(devices)])]
    ppermute x0 -> x25, waiting for transfers between devices: none -> 30.8 us  [swap(): return lax.ppermute(x, 'ctx', [(d, d ^ bits) for d in range(devices)])]
    dot_general x5 -> x0, matrix products: 26.4 us -> none  [the longest x1 18.6 us: body(): lax.dot_general(out_weight, mixed, (((0,), (1,)), ((), ())), preferred_el...]
    all_to_all x4 -> x0, starting transfers between devices: 19.9 us -> none  [the longest x1 7.41 us: body(): lax.all_to_all(keys_by_head[target], 'ctx', split_axis=0, concat_axis=0,...]
    pallas_call x0 -> x17, Pallas kernels: none -> 17.7 us  [the longest x1 6.22 us: attend(): pl.pallas_call(attention_kernel, out_shape=shape((count, heads * HD)), in...]
    gather x9 -> x0, local copies, waits for them, and re-layouts: 9.32 us -> none  [the longest x1 1.44 us: body(): values_by_head[target]]
  transfers between devices with their start and end apart: 5 -> 25, of which waited for: 5 -> 9; matrix products, arithmetic and copies ran while one was open for 11% -> 0% of each run, Pallas kernels for 0% -> 8%
where the time goes in v1:
time: 94.9 us; the launch traced here: 94.7 us
  starting transfers between devices  34.2 us (36%)
  waiting for transfers between devices  30.8 us (32%)
  Pallas kernels  17.7 us (19%)
  local copies, waits for them, and re-layouts  11.2 us (12%)
    ppermute x25, starting transfers between devices, swap(): return lax.ppermute(x, 'ctx', [(d, d ^ bits) for d in range(devices)])  34.2 us
    ppermute x25, waiting for transfers between devices, swap(): return lax.ppermute(x, 'ctx', [(d, d ^ bits) for d in range(devices)])  30.8 us
    unnamed x6, local copies, waits for them, and re-layouts  11.2 us
    pallas_call x1, Pallas kernels, attend(): pl.pallas_call(attention_kernel, out_shape=shape((count, heads * HD)), in...  6.22 us
    pallas_call x2, Pallas kernels, project_keep(): pl.pallas_call(lambda *refs: project_keep_kernel(masks, start, *refs), ou...  2.62 us
    pallas_call x2, Pallas kernels, project_send(): pl.pallas_call(lambda *refs: project_send_kernel(masks, start, *refs), ou...  2.57 us
  transfers between devices with their start and end apart: 25, of which 9 were waited for; matrix products, arithmetic and copies ran while one was open for 0% of the time, Pallas kernels for 8%

profile of v1, /device:TPU:0, one launch (start us, length us, event | category | flops | bytes accessed | tf_op | source)
XLA Modules:
  0.0 94.7 jit_solution(7238210927662756467)
XLA Ops:
  0.6 1.7 %prepare_rows.1 = (bf16[2,128,128]{2,1,0:T(8,128)(2,1)S(1)}, bf16[2,128,128]{2,1,0:T(8,128)(2,1)S(1)}, bf16[2,128,128]{2,1,0:T(8,128)(2,1)S(1)}, bf16[2,128,128]...) custom-call(s32[1]{0:T(128)} %bitcast.here_ref.refs_0_, ...), custom_call_target="tpu_custom_call" | custom-call | flops 2621440 | bytes 1048576 | tf_op jit(solution)/shard_map/prepare_rows/pallas_call | solution.py:128
  2.4 3.1 %collective-permute-start = (bf16[2,128,128]{2,1,0:T(8,128)(2,1)S(1)}, bf16[2,128,128]{2,1,0:T(8,128)(2,1)S(1)}, u32[]{:S(2)}, u32[]{:S(2)}) collective-permute-start(bf16[2,128,128]{2,1,0:T(8,128)(2,1)S(1)} %get-tuple-element.41), channel_id=1, source_target_pairs={{0,2},{1,3},{2,0},{3,1},{4,6},{5,7},{6,4},{7,5},{8,10},{9,11},{10,... | collective-permute-start | bytes 196616 | tf_op jit(solution)/shard_map/ppermute | solution.py:456
  5.4 1.6 %collective-permute-start.1 = (bf16[2,128,128]{2,1,0:T(8,128)(2,1)S(1)}, bf16[2,128,128]{2,1,0:T(8,128)(2,1)S(1)}, u32[]{:S(2)}, u32[]{:S(2)}) collective-permute-start(bf16[2,128,128]{2,1,0:T(8,128)(2,1)S(1)} %get-tuple-element.42), channel_id=1, source_target_pairs={{0,4},{1,5},{2,6},{3,7},{4,0},{5,1},{6,2},{7,3},{8,12},{9,13},{10,... | collective-permute-start | bytes 196616 | tf_op jit(solution)/shard_map/ppermute | solution.py:456
  7.0 3.0 %collective-permute-start.3 = (bf16[2,128,128]{2,1,0:T(8,128)(2,1)S(1)}, bf16[2,128,128]{2,1,0:T(8,128)(2,1)S(1)}, u32[]{:S(2)}, u32[]{:S(2)}) collective-permute-start(bf16[2,128,128]{2,1,0:T(8,128)(2,1)S(1)} %get-tuple-element.44), channel_id=1, source_target_pairs={{0,8},{1,9},{2,10},{3,11},{4,12},{5,13},{6,14},{7,15},{8,0},{9,1},... | collective-permute-start | bytes 196616 | tf_op jit(solution)/shard_map/ppermute | solution.py:456
  10.0 1.3 %collective-permute-start.4 = (bf16[2,128,128]{2,1,0:T(8,128)(2,1)S(1)}, bf16[2,128,128]{2,1,0:T(8,128)(2,1)S(1)}, u32[]{:S(2)}, u32[]{:S(2)}) collective-permute-start(bf16[2,128,128]{2,1,0:T(8,128)(2,1)S(1)} %get-tuple-element.45), channel_id=1, source_target_pairs={{0,10},{1,11},{2,8},{3,9},{4,14},{5,15},{6,12},{7,13},{8,2},{9,3},... | collective-permute-start | bytes 196616 | tf_op jit(solution)/shard_map/ppermute | solution.py:456
  11.3 3.6 %collective-permute-start.5 = (bf16[2,128,128]{2,1,0:T(8,128)(2,1)S(1)}, bf16[2,128,128]{2,1,0:T(8,128)(2,1)S(1)}, u32[]{:S(2)}, u32[]{:S(2)}) collective-permute-start(bf16[2,128,128]{2,1,0:T(8,128)(2,1)S(1)} %get-tuple-element.46), channel_id=1, source_target_pairs={{0,12},{1,13},{2,14},{3,15},{4,8},{5,9},{6,10},{7,11},{8,4},{9,5},... | collective-permute-start | bytes 196616 | tf_op jit(solution)/shard_map/ppermute | solution.py:456
  15.0 5.2 %collective-permute-done.4.refs_1_ = bf16[2,128,128]{2,1,0:T(8,128)(2,1)S(1)} collective-permute-done((bf16[2,128,128]{2,1,0:T(8,128)(2,1)S(1)}, bf16[2,128,128]{2,1,0:T(8,128)(2,1)S(1)}, u32[]{:S(2)}, u32[]{:S(2)}) %collective-permute-start.4) | collective-permute-done | bytes 65568 | tf_op jit(solution)/shard_map/ppermute | solution.py:456
  20.2 1.7 %collective-permute-done.6.refs_3_ = bf16[2,128,128]{2,1,0:T(8,128)(2,1)S(1)} collective-permute-done((bf16[2,128,128]{2,1,0:T(8,128)(2,1)S(1)}, bf16[2,128,128]{2,1,0:T(8,128)(2,1)S(1)}, u32[]{:S(2)}, u32[]{:S(2)}) %collective-permute-start.6) | collective-permute-done | bytes 65568 | tf_op jit(solution)/shard_map/ppermute | solution.py:456
  22.1 1.6 %side.1 = (bf16[1024,128]{1,0:T(8,128)(2,1)S(1)}, f32[1,2048]{1,0:T(1,128)S(1)}) custom-call(s32[1]{0:T(128)} %bitcast.here_ref.refs_0_, f32[2,128]{1,0:T(2,128)} %constant.6.clone.refs_2_.refs_0_, s32[1,128]{1,0:T(1,128)} %bitcast.6, s32[1,128]{1,0:T(1,128)} %bitcast.10, s32[1,128]{1,0:T(1,128)} %bitcast.12, s32[1,128]{1,0:T(1,128)} %bitcast.7, ...), custom_call_target="tpu_custom_call" | custom-call | flops 1048576 | bytes 67108864 | tf_op jit(solution)/shard_map/side/pallas_call | solution.py:171
  24.4 6.2 %attend.1.refs_1_ = bf16[128,1024]{1,0:T(8,128)(2,1)S(1)} custom-call(bf16[4,2,128,128]{3,2,1,0:T(8,128)(2,1)S(1)} %shard_map.139.refs_0_, bf16[4,2,128,128]{3,2,1,0:T(8,128)(2,1)S(1)} %shard_map.140.refs_1_, bf16[4,2,128,128]{3,2,1,0:T(8,128)(2,1)S(1)} %collective-permute-done.7.refs_2_, bf16[4,2,128,128]{3,2,1,0:T(8,128)(2,1)S(1)} %collective-permute-done.8.refs_3_, ...), custom_call_target="tpu_custom_call" | custom-call | flops 1073741824 | bytes 1048576 | tf_op jit(solution)/shard_map/attend/pallas_call | solution.py:332
  30.6 10.5 %copy-done = bf16[1024,16384]{1,0:T(8,128)(2,1)S(1)} copy-done((bf16[1024,16384]{1,0:T(8,128)(2,1)S(1)}, bf16[1024,16384]{1,0:T(8,128)(2,1)}, u32[]{:S(2)}) %copy-start) | copy-done | bytes 33554456
  41.1 1.3 %shard_map.141 = bf16[8,128,512]{2,1,0:T(8,128)(2,1)S(1)} custom-call(s32[1]{0:T(128)} %bitcast.here_ref.refs_0_, bf16[128,1024]{1,0:T(8,128)(2,1)S(1)} %attend.1.refs_1_, bf16[1024,16384]{1,0:T(8,128)(2,1)S(1)} %copy-done), custom_call_target="tpu_custom_call" | custom-call | flops 1073741824 | bytes 8388608 | tf_op jit(solution)/shard_map/pallas_call | solution.py:385
  43.0 1.3 %shard_map.142 = bf16[8,128,512]{2,1,0:T(8,128)(2,1)S(1)} custom-call(s32[1]{0:T(128)} %bitcast.here_ref.refs_0_, bf16[128,1024]{1,0:T(8,128)(2,1)S(1)} %attend.1.refs_1_, bf16[1024,16384]{1,0:T(8,128)(2,1)S(1)} %copy-done), custom_call_target="tpu_custom_call" | custom-call | flops 1073741824 | bytes 8388608 | tf_op jit(solution)/shard_map/pallas_call | solution.py:385
  44.4 0.9 collective-permute-done.17.refs_3_
  45.3 1.3 %shard_map.143 = (bf16[4,128,512]{2,1,0:T(8,128)(2,1)S(1)}, f32[4,128,512]{2,1,0:T(8,128)S(1)}) custom-call(s32[1]{0:T(128)} %bitcast.here_ref.refs_0_, bf16[128,1024]{1,0:T(8,128)(2,1)S(1)} %attend.1.refs_1_, bf16[1024,16384]{1,0:T(8,128)(2,1)S(1)} %copy-done, bf16[8,128,512]{2,1,0:T(8,128)(2,1)S(1)} %collective-permute-done.17.refs_3_), custom_call_target="tpu_custom_call" | custom-call | flops 1073741824 | bytes 8388608 | tf_op jit(solution)/shard_map/pallas_call | solution.py:398
  47.1 1.4 %shard_map.146 = (bf16[4,128,512]{2,1,0:T(8,128)(2,1)S(1)}, f32[4,128,512]{2,1,0:T(8,128)S(1)}) custom-call(s32[1]{0:T(128)} %bitcast.here_ref.refs_0_, bf16[128,1024]{1,0:T(8,128)(2,1)S(1)} %attend.1.refs_1_, bf16[1024,16384]{1,0:T(8,128)(2,1)S(1)} %copy-done, bf16[8,128,512]{2,1,0:T(8,128)(2,1)S(1)} %collective-permute-done.21.refs_3_), custom_call_target="tpu_custom_call" | custom-call | flops 1073741824 | bytes 8388608 | tf_op jit(solution)/shard_map/pallas_call | solution.py:398
  48.5 2.0 %collective-permute-start.22 = (bf16[4,128,512]{2,1,0:T(8,128)(2,1)S(1)}, bf16[4,128,512]{2,1,0:T(8,128)(2,1)S(1)}, u32[]{:S(2)}, u32[]{:S(2)}) collective-permute-start(bf16[4,128,512]{2,1,0:T(8,128)(2,1)S(1)} %get-tuple-element.72), channel_id=1, source_target_pairs={{0,4},{1,5},{2,6},{3,7},{4,0},{5,1},{6,2},{7,3},{8,12},{9,13},{10,... | collective-permute-start | bytes 1572872 | tf_op jit(solution)/shard_map/ppermute | solution.py:456
  50.5 0.9 order_pages.1
  51.4 1.3 %collective-permute-start.9 = (bf16[16,16,128]{2,1,0:T(8,128)(2,1)S(1)}, bf16[16,16,128]{2,1,0:T(8,128)(2,1)S(1)}, u32[]{:S(2)}, u32[]{:S(2)}) collective-permute-start(bf16[16,16,128]{2,1,0:T(8,128)(2,1)S(1)} %get-tuple-element.49), channel_id=1, source_target_pairs={{0,2},{1,3},{2,0},{3,1},{4,6},{5,7},{6,4},{7,5},{8,10},{9,11},{10,... | collective-permute-start | bytes 196616 | tf_op jit(solution)/shard_map/ppermute | solution.py:456
  53.0 1.9 %collective-permute-start.11 = (bf16[16,16,128]{2,1,0:T(8,128)(2,1)S(1)}, bf16[16,16,128]{2,1,0:T(8,128)(2,1)S(1)}, u32[]{:S(2)}, u32[]{:S(2)}) collective-permute-start(bf16[16,16,128]{2,1,0:T(8,128)(2,1)S(1)} %get-tuple-element.51), channel_id=1, source_target_pairs={{0,6},{1,7},{2,4},{3,5},{4,2},{5,3},{6,0},{7,1},{8,14},{9,15},{10,... | collective-permute-start | bytes 196616 | tf_op jit(solution)/shard_map/ppermute | solution.py:456
  54.9 6.5 %collective-permute-done.18.got_ref = bf16[4,128,512]{2,1,0:T(8,128)(2,1)S(1)} collective-permute-done((bf16[4,128,512]{2,1,0:T(8,128)(2,1)S(1)}, bf16[4,128,512]{2,1,0:T(8,128)(2,1)S(1)}, u32[]{:S(2)}, u32[]{:S(2)}) %collective-permute-start.18) | collective-permute-done | bytes 524320 | tf_op jit(solution)/shard_map/ppermute | solution.py:456
  61.4 2.8 %collective-permute-start.12 = (bf16[16,16,128]{2,1,0:T(8,128)(2,1)S(1)}, bf16[16,16,128]{2,1,0:T(8,128)(2,1)S(1)}, u32[]{:S(2)}, u32[]{:S(2)}) collective-permute-start(bf16[16,16,128]{2,1,0:T(8,128)(2,1)S(1)} %get-tuple-element.52), channel_id=1, source_target_pairs={{0,8},{1,9},{2,10},{3,11},{4,12},{5,13},{6,14},{7,15},{8,0},{9,1},... | collective-permute-start | bytes 196616 | tf_op jit(solution)/shard_map/ppermute | solution.py:456
  64.3 1.0 %collective-permute-start.19 = (bf16[2,128,512]{2,1,0:T(8,128)(2,1)S(1)}, bf16[2,128,512]{2,1,0:T(8,128)(2,1)S(1)}, u32[]{:S(2)}, u32[]{:S(2)}) collective-permute-start(bf16[2,128,512]{2,1,0:T(8,128)(2,1)S(1)} %get-tuple-element.67), channel_id=1, source_target_pairs={{0,4},{1,5},{2,6},{3,7},{4,0},{5,1},{6,2},{7,3},{8,12},{9,13},{10,... | collective-permute-start | bytes 786440 | tf_op jit(solution)/shard_map/ppermute | solution.py:456
  65.4 1.3 %collective-permute-start.23 = (bf16[2,128,512]{2,1,0:T(8,128)(2,1)S(1)}, bf16[2,128,512]{2,1,0:T(8,128)(2,1)S(1)}, u32[]{:S(2)}, u32[]{:S(2)}) collective-permute-start(bf16[2,128,512]{2,1,0:T(8,128)(2,1)S(1)} %get-tuple-element.74), channel_id=1, source_target_pairs={{0,2},{1,3},{2,0},{3,1},{4,6},{5,7},{6,4},{7,5},{8,10},{9,11},{10,... | collective-permute-start | bytes 786440 | tf_op jit(solution)/shard_map/ppermute | solution.py:456
  66.7 1.8 %collective-permute-start.13 = (bf16[16,16,128]{2,1,0:T(8,128)(2,1)S(1)}, bf16[16,16,128]{2,1,0:T(8,128)(2,1)S(1)}, u32[]{:S(2)}, u32[]{:S(2)}) collective-permute-start(bf16[16,16,128]{2,1,0:T(8,128)(2,1)S(1)} %get-tuple-element.53), channel_id=1, source_target_pairs={{0,10},{1,11},{2,8},{3,9},{4,14},{5,15},{6,12},{7,13},{8,2},{9,3},... | collective-permute-start | bytes 196616 | tf_op jit(solution)/shard_map/ppermute | solution.py:456
  68.5 2.2 %collective-permute-start.14 = (bf16[16,16,128]{2,1,0:T(8,128)(2,1)S(1)}, bf16[16,16,128]{2,1,0:T(8,128)(2,1)S(1)}, u32[]{:S(2)}, u32[]{:S(2)}) collective-permute-start(bf16[16,16,128]{2,1,0:T(8,128)(2,1)S(1)} %get-tuple-element.54), channel_id=1, source_target_pairs={{0,12},{1,13},{2,14},{3,15},{4,8},{5,9},{6,10},{7,11},{8,4},{9,5},... | collective-permute-start | bytes 196616 | tf_op jit(solution)/shard_map/ppermute | solution.py:456
  70.7 2.6 %collective-permute-start.15 = (bf16[16,16,128]{2,1,0:T(8,128)(2,1)S(1)}, bf16[16,16,128]{2,1,0:T(8,128)(2,1)S(1)}, u32[]{:S(2)}, u32[]{:S(2)}) collective-permute-start(bf16[16,16,128]{2,1,0:T(8,128)(2,1)S(1)} %get-tuple-element.55), channel_id=1, source_target_pairs={{0,14},{1,15},{2,12},{3,13},{4,10},{5,11},{6,8},{7,9},{8,6},{9,7},... | collective-permute-start | bytes 196616 | tf_op jit(solution)/shard_map/ppermute | solution.py:456
  74.1 4.0 %collective-permute-done.14.refs_6_ = bf16[16,16,128]{2,1,0:T(8,128)(2,1)S(1)} collective-permute-done((bf16[16,16,128]{2,1,0:T(8,128)(2,1)S(1)}, bf16[16,16,128]{2,1,0:T(8,128)(2,1)S(1)}, u32[]{:S(2)}, u32[]{:S(2)}) %collective-permute-start.14) | collective-permute-done | bytes 65568 | tf_op jit(solution)/shard_map/ppermute | solution.py:456
  78.1 1.6 %collective-permute-done.15.refs_7_ = bf16[16,16,128]{2,1,0:T(8,128)(2,1)S(1)} collective-permute-done((bf16[16,16,128]{2,1,0:T(8,128)(2,1)S(1)}, bf16[16,16,128]{2,1,0:T(8,128)(2,1)S(1)}, u32[]{:S(2)}, u32[]{:S(2)}) %collective-permute-start.15) | collective-permute-done | bytes 65568 | tf_op jit(solution)/shard_map/ppermute | solution.py:456
  80.7 2.4 %collective-permute-start.24 = (bf16[1,128,512]{2,1,0:T(8,128)(2,1)S(1)}, bf16[1,128,512]{2,1,0:T(8,128)(2,1)S(1)}, u32[]{:S(2)}, u32[]{:S(2)}) collective-permute-start(bf16[1,128,512]{2,1,0:T(8,128)(2,1)S(1)} %get-tuple-element.76), channel_id=1, source_target_pairs={{0,8},{1,9},{2,10},{3,11},{4,12},{5,13},{6,14},{7,15},{8,0},{9,1},... | collective-permute-start | bytes 393224 | tf_op jit(solution)/shard_map/ppermute | solution.py:456
  83.9 7.3 %collective-permute-done.20.refs_1_ = bf16[1,128,512]{2,1,0:T(8,128)(2,1)S(1)} collective-permute-done((bf16[1,128,512]{2,1,0:T(8,128)(2,1)S(1)}, bf16[1,128,512]{2,1,0:T(8,128)(2,1)S(1)}, u32[]{:S(2)}, u32[]{:S(2)}) %collective-permute-start.20) | collective-permute-done | bytes 131104 | tf_op jit(solution)/shard_map/ppermute | solution.py:456
  91.2 2.8 %collective-permute-done.24.refs_3_ = bf16[1,128,512]{2,1,0:T(8,128)(2,1)S(1)} collective-permute-done((bf16[1,128,512]{2,1,0:T(8,128)(2,1)S(1)}, bf16[1,128,512]{2,1,0:T(8,128)(2,1)S(1)}, u32[]{:S(2)}, u32[]{:S(2)}) %collective-permute-start.24) | collective-permute-done | bytes 131104 | tf_op jit(solution)/shard_map/ppermute | solution.py:456
  (41 shorter events, 6.1 us)
Async XLA Ops:
  2.4 8.9 %collective-permute-start = (bf16[2,128,128]{2,1,0:T(8,128)(2,1)S(1)}, bf16[2,128,128]{2,1,0:T(8,128)(2,1)S(1)}, u32[]{:S(2)}, u32[]{:S(2)}) collective-permute-start(bf16[2,128,128]{2,1,0:T(8,128)(2,1)S(1)} %get-tuple-element.41), channel_id=1, source_target_pairs={{0,2},{1,3},{2,0},{3,1},{4,6},{5,7},{6,4},{7,5},{8,10},{9,11},{10,... | collective-permute-start | bytes 196616 | tf_op jit(solution)/shard_map/ppermute | solution.py:456
  5.4 9.5 %collective-permute-start.1 = (bf16[2,128,128]{2,1,0:T(8,128)(2,1)S(1)}, bf16[2,128,128]{2,1,0:T(8,128)(2,1)S(1)}, u32[]{:S(2)}, u32[]{:S(2)}) collective-permute-start(bf16[2,128,128]{2,1,0:T(8,128)(2,1)S(1)} %get-tuple-element.42), channel_id=1, source_target_pairs={{0,4},{1,5},{2,6},{3,7},{4,0},{5,1},{6,2},{7,3},{8,12},{9,13},{10,... | collective-permute-start | bytes 196616 | tf_op jit(solution)/shard_map/ppermute | solution.py:456
  7.0 7.9 %collective-permute-start.2 = (bf16[2,128,128]{2,1,0:T(8,128)(2,1)S(1)}, bf16[2,128,128]{2,1,0:T(8,128)(2,1)S(1)}, u32[]{:S(2)}, u32[]{:S(2)}) collective-permute-start(bf16[2,128,128]{2,1,0:T(8,128)(2,1)S(1)} %get-tuple-element.43), channel_id=1, source_target_pairs={{0,6},{1,7},{2,4},{3,5},{4,2},{5,3},{6,0},{7,1},{8,14},{9,15},{10,... | collective-permute-start | bytes 196616 | tf_op jit(solution)/shard_map/ppermute | solution.py:456
  7.0 8.0 %collective-permute-start.3 = (bf16[2,128,128]{2,1,0:T(8,128)(2,1)S(1)}, bf16[2,128,128]{2,1,0:T(8,128)(2,1)S(1)}, u32[]{:S(2)}, u32[]{:S(2)}) collective-permute-start(bf16[2,128,128]{2,1,0:T(8,128)(2,1)S(1)} %get-tuple-element.44), channel_id=1, source_target_pairs={{0,8},{1,9},{2,10},{3,11},{4,12},{5,13},{6,14},{7,15},{8,0},{9,1},... | collective-permute-start | bytes 196616 | tf_op jit(solution)/shard_map/ppermute | solution.py:456
  10.0 10.2 %collective-permute-start.4 = (bf16[2,128,128]{2,1,0:T(8,128)(2,1)S(1)}, bf16[2,128,128]{2,1,0:T(8,128)(2,1)S(1)}, u32[]{:S(2)}, u32[]{:S(2)}) collective-permute-start(bf16[2,128,128]{2,1,0:T(8,128)(2,1)S(1)} %get-tuple-element.45), channel_id=1, source_target_pairs={{0,10},{1,11},{2,8},{3,9},{4,14},{5,15},{6,12},{7,13},{8,2},{9,3},... | collective-permute-start | bytes 196616 | tf_op jit(solution)/shard_map/ppermute | solution.py:456
  11.3 8.9 %collective-permute-start.5 = (bf16[2,128,128]{2,1,0:T(8,128)(2,1)S(1)}, bf16[2,128,128]{2,1,0:T(8,128)(2,1)S(1)}, u32[]{:S(2)}, u32[]{:S(2)}) collective-permute-start(bf16[2,128,128]{2,1,0:T(8,128)(2,1)S(1)} %get-tuple-element.46), channel_id=1, source_target_pairs={{0,12},{1,13},{2,14},{3,15},{4,8},{5,9},{6,10},{7,11},{8,4},{9,5},... | collective-permute-start | bytes 196616 | tf_op jit(solution)/shard_map/ppermute | solution.py:456
  14.9 7.1 %collective-permute-start.6 = (bf16[2,128,128]{2,1,0:T(8,128)(2,1)S(1)}, bf16[2,128,128]{2,1,0:T(8,128)(2,1)S(1)}, u32[]{:S(2)}, u32[]{:S(2)}) collective-permute-start(bf16[2,128,128]{2,1,0:T(8,128)(2,1)S(1)} %get-tuple-element.47), channel_id=1, source_target_pairs={{0,14},{1,15},{2,12},{3,13},{4,10},{5,11},{6,8},{7,9},{8,6},{9,7},... | collective-permute-start | bytes 196616 | tf_op jit(solution)/shard_map/ppermute | solution.py:456
  14.9 8.8 %collective-permute-start.7 = (bf16[4,2,128,128]{3,2,1,0:T(8,128)(2,1)S(1)}, bf16[4,2,128,128]{3,2,1,0:T(8,128)(2,1)S(1)}, u32[]{:S(2)}, u32[]{:S(2)}) collective-permute-start(bf16[4,2,128,128]{3,2,1,0:T(8,128)(2,1)S(1)} %shard_map.139.refs_0_), channel_id=1, source_target_pairs={{0,1},{1,0},{2,3},{3,2},{4,5},{5,4},{6,7},{7,6},{8,9},{9,8},{10,11... | collective-permute-start | bytes 786440 | tf_op jit(solution)/shard_map/ppermute | solution.py:456
  22.0 1.7 %collective-permute-start.8 = (bf16[4,2,128,128]{3,2,1,0:T(8,128)(2,1)S(1)}, bf16[4,2,128,128]{3,2,1,0:T(8,128)(2,1)S(1)}, u32[]{:S(2)}, u32[]{:S(2)}) collective-permute-start(bf16[4,2,128,128]{3,2,1,0:T(8,128)(2,1)S(1)} %shard_map.140.refs_1_), channel_id=1, source_target_pairs={{0,1},{1,0},{2,3},{3,2},{4,5},{5,4},{6,7},{7,6},{8,9},{9,8},{10,11... | collective-permute-start | bytes 786440 | tf_op jit(solution)/shard_map/ppermute | solution.py:456
  23.7 0.7 copy-start.2
  30.6 10.5 %copy-start = (bf16[1024,16384]{1,0:T(8,128)(2,1)S(1)}, bf16[1024,16384]{1,0:T(8,128)(2,1)}, u32[]{:S(2)}) copy-start(bf16[1024,16384]{1,0:T(8,128)(2,1)} %refs_2_.8) | copy-start | bytes 100663296
  42.4 2.8 %collective-permute-start.17 = (bf16[8,128,512]{2,1,0:T(8,128)(2,1)S(1)}, bf16[8,128,512]{2,1,0:T(8,128)(2,1)S(1)}, u32[]{:S(2)}, u32[]{:S(2)}) collective-permute-start(bf16[8,128,512]{2,1,0:T(8,128)(2,1)S(1)} %shard_map.141), channel_id=1, source_target_pairs={{0,1},{1,0},{2,3},{3,2},{4,5},{5,4},{6,7},{7,6},{8,9},{9,8},{10,11... | collective-permute-start | bytes 3145736 | tf_op jit(solution)/shard_map/ppermute | solution.py:456
  44.3 6.2 %copy-start.1 = (s32[128]{0:T(128)S(1)}, s32[128]{0:T(128)}, u32[]{:S(2)}) copy-start(s32[128]{0:T(128)} %source_ref.1) | copy-start | bytes 1540
  44.3 2.8 %collective-permute-start.21 = (bf16[8,128,512]{2,1,0:T(8,128)(2,1)S(1)}, bf16[8,128,512]{2,1,0:T(8,128)(2,1)S(1)}, u32[]{:S(2)}, u32[]{:S(2)}) collective-permute-start(bf16[8,128,512]{2,1,0:T(8,128)(2,1)S(1)} %shard_map.142), channel_id=1, source_target_pairs={{0,1},{1,0},{2,3},{3,2},{4,5},{5,4},{6,7},{7,6},{8,9},{9,8},{10,11... | collective-permute-start | bytes 3145736 | tf_op jit(solution)/shard_map/ppermute | solution.py:456
  46.5 14.9 %collective-permute-start.18 = (bf16[4,128,512]{2,1,0:T(8,128)(2,1)S(1)}, bf16[4,128,512]{2,1,0:T(8,128)(2,1)S(1)}, u32[]{:S(2)}, u32[]{:S(2)}) collective-permute-start(bf16[4,128,512]{2,1,0:T(8,128)(2,1)S(1)} %get-tuple-element.65), channel_id=1, source_target_pairs={{0,2},{1,3},{2,0},{3,1},{4,6},{5,7},{6,4},{7,5},{8,10},{9,11},{10,... | collective-permute-start | bytes 1572872 | tf_op jit(solution)/shard_map/ppermute | solution.py:456
  48.5 15.8 %collective-permute-start.22 = (bf16[4,128,512]{2,1,0:T(8,128)(2,1)S(1)}, bf16[4,128,512]{2,1,0:T(8,128)(2,1)S(1)}, u32[]{:S(2)}, u32[]{:S(2)}) collective-permute-start(bf16[4,128,512]{2,1,0:T(8,128)(2,1)S(1)} %get-tuple-element.72), channel_id=1, source_target_pairs={{0,4},{1,5},{2,6},{3,7},{4,0},{5,1},{6,2},{7,3},{8,12},{9,13},{10,... | collective-permute-start | bytes 1572872 | tf_op jit(solution)/shard_map/ppermute | solution.py:456
  51.4 14.1 %collective-permute-start.9 = (bf16[16,16,128]{2,1,0:T(8,128)(2,1)S(1)}, bf16[16,16,128]{2,1,0:T(8,128)(2,1)S(1)}, u32[]{:S(2)}, u32[]{:S(2)}) collective-permute-start(bf16[16,16,128]{2,1,0:T(8,128)(2,1)S(1)} %get-tuple-element.49), channel_id=1, source_target_pairs={{0,2},{1,3},{2,0},{3,1},{4,6},{5,7},{6,4},{7,5},{8,10},{9,11},{10,... | collective-permute-start | bytes 196616 | tf_op jit(solution)/shard_map/ppermute | solution.py:456
  52.6 14.1 %collective-permute-start.10 = (bf16[16,16,128]{2,1,0:T(8,128)(2,1)S(1)}, bf16[16,16,128]{2,1,0:T(8,128)(2,1)S(1)}, u32[]{:S(2)}, u32[]{:S(2)}) collective-permute-start(bf16[16,16,128]{2,1,0:T(8,128)(2,1)S(1)} %get-tuple-element.50), channel_id=1, source_target_pairs={{0,4},{1,5},{2,6},{3,7},{4,0},{5,1},{6,2},{7,3},{8,12},{9,13},{10,... | collective-permute-start | bytes 196616 | tf_op jit(solution)/shard_map/ppermute | solution.py:456
  53.0 15.5 %collective-permute-start.11 = (bf16[16,16,128]{2,1,0:T(8,128)(2,1)S(1)}, bf16[16,16,128]{2,1,0:T(8,128)(2,1)S(1)}, u32[]{:S(2)}, u32[]{:S(2)}) collective-permute-start(bf16[16,16,128]{2,1,0:T(8,128)(2,1)S(1)} %get-tuple-element.51), channel_id=1, source_target_pairs={{0,6},{1,7},{2,4},{3,5},{4,2},{5,3},{6,0},{7,1},{8,14},{9,15},{10,... | collective-permute-start | bytes 196616 | tf_op jit(solution)/shard_map/ppermute | solution.py:456
  61.4 9.3 %collective-permute-start.12 = (bf16[16,16,128]{2,1,0:T(8,128)(2,1)S(1)}, bf16[16,16,128]{2,1,0:T(8,128)(2,1)S(1)}, u32[]{:S(2)}, u32[]{:S(2)}) collective-permute-start(bf16[16,16,128]{2,1,0:T(8,128)(2,1)S(1)} %get-tuple-element.52), channel_id=1, source_target_pairs={{0,8},{1,9},{2,10},{3,11},{4,12},{5,13},{6,14},{7,15},{8,0},{9,1},... | collective-permute-start | bytes 196616 | tf_op jit(solution)/shard_map/ppermute | solution.py:456
  64.3 15.6 %collective-permute-start.19 = (bf16[2,128,512]{2,1,0:T(8,128)(2,1)S(1)}, bf16[2,128,512]{2,1,0:T(8,128)(2,1)S(1)}, u32[]{:S(2)}, u32[]{:S(2)}) collective-permute-start(bf16[2,128,512]{2,1,0:T(8,128)(2,1)S(1)} %get-tuple-element.67), channel_id=1, source_target_pairs={{0,4},{1,5},{2,6},{3,7},{4,0},{5,1},{6,2},{7,3},{8,12},{9,13},{10,... | collective-permute-start | bytes 786440 | tf_op jit(solution)/shard_map/ppermute | solution.py:456
  65.4 15.2 %collective-permute-start.23 = (bf16[2,128,512]{2,1,0:T(8,128)(2,1)S(1)}, bf16[2,128,512]{2,1,0:T(8,128)(2,1)S(1)}, u32[]{:S(2)}, u32[]{:S(2)}) collective-permute-start(bf16[2,128,512]{2,1,0:T(8,128)(2,1)S(1)} %get-tuple-element.74), channel_id=1, source_target_pairs={{0,2},{1,3},{2,0},{3,1},{4,6},{5,7},{6,4},{7,5},{8,10},{9,11},{10,... | collective-permute-start | bytes 786440 | tf_op jit(solution)/shard_map/ppermute | solution.py:456
  66.7 7.4 %collective-permute-start.13 = (bf16[16,16,128]{2,1,0:T(8,128)(2,1)S(1)}, bf16[16,16,128]{2,1,0:T(8,128)(2,1)S(1)}, u32[]{:S(2)}, u32[]{:S(2)}) collective-permute-start(bf16[16,16,128]{2,1,0:T(8,128)(2,1)S(1)} %get-tuple-element.53), channel_id=1, source_target_pairs={{0,10},{1,11},{2,8},{3,9},{4,14},{5,15},{6,12},{7,13},{8,2},{9,3},... | collective-permute-start | bytes 196616 | tf_op jit(solution)/shard_map/ppermute | solution.py:456
  68.5 9.6 %collective-permute-start.14 = (bf16[16,16,128]{2,1,0:T(8,128)(2,1)S(1)}, bf16[16,16,128]{2,1,0:T(8,128)(2,1)S(1)}, u32[]{:S(2)}, u32[]{:S(2)}) collective-permute-start(bf16[16,16,128]{2,1,0:T(8,128)(2,1)S(1)} %get-tuple-element.54), channel_id=1, source_target_pairs={{0,12},{1,13},{2,14},{3,15},{4,8},{5,9},{6,10},{7,11},{8,4},{9,5},... | collective-permute-start | bytes 196616 | tf_op jit(solution)/shard_map/ppermute | solution.py:456
  70.7 8.9 %collective-permute-start.15 = (bf16[16,16,128]{2,1,0:T(8,128)(2,1)S(1)}, bf16[16,16,128]{2,1,0:T(8,128)(2,1)S(1)}, u32[]{:S(2)}, u32[]{:S(2)}) collective-permute-start(bf16[16,16,128]{2,1,0:T(8,128)(2,1)S(1)} %get-tuple-element.55), channel_id=1, source_target_pairs={{0,14},{1,15},{2,12},{3,13},{4,10},{5,11},{6,8},{7,9},{8,6},{9,7},... | collective-permute-start | bytes 196616 | tf_op jit(solution)/shard_map/ppermute | solution.py:456
  79.8 3.3 %collective-permute-start.16 = (bf16[128,1024]{1,0:T(8,128)(2,1)S(1)}, bf16[128,1024]{1,0:T(8,128)(2,1)S(1)}, u32[]{:S(2)}, u32[]{:S(2)}) collective-permute-start(bf16[128,1024]{1,0:T(8,128)(2,1)S(1)} %get-tuple-element.57), channel_id=1, source_target_pairs={{0,1},{1,0},{2,3},{3,2},{4,5},{5,4},{6,7},{7,6},{8,9},{9,8},{10,11... | collective-permute-start | bytes 786440 | tf_op jit(solution)/shard_map/ppermute | solution.py:456
  80.0 11.2 %collective-permute-start.20 = (bf16[1,128,512]{2,1,0:T(8,128)(2,1)S(1)}, bf16[1,128,512]{2,1,0:T(8,128)(2,1)S(1)}, u32[]{:S(2)}, u32[]{:S(2)}) collective-permute-start(bf16[1,128,512]{2,1,0:T(8,128)(2,1)S(1)} %get-tuple-element.69), channel_id=1, source_target_pairs={{0,8},{1,9},{2,10},{3,11},{4,12},{5,13},{6,14},{7,15},{8,0},{9,1},... | collective-permute-start | bytes 393224 | tf_op jit(solution)/shard_map/ppermute | solution.py:456
  80.7 13.2 %collective-permute-start.24 = (bf16[1,128,512]{2,1,0:T(8,128)(2,1)S(1)}, bf16[1,128,512]{2,1,0:T(8,128)(2,1)S(1)}, u32[]{:S(2)}, u32[]{:S(2)}) collective-permute-start(bf16[1,128,512]{2,1,0:T(8,128)(2,1)S(1)} %get-tuple-element.76), channel_id=1, source_target_pairs={{0,8},{1,9},{2,10},{3,11},{4,12},{5,13},{6,14},{7,15},{8,0},{9,1},... | collective-permute-start | bytes 393224 | tf_op jit(solution)/shard_map/ppermute | solution.py:456

commit v2 on v1

--- a/solution.py
+++ b/solution.py
@@ -14,6 +14,8 @@
 HD = 128
 PAGE = 16
 MIB = 1 << 20
+UNROLL = 1
+EARLY = 12
 
 
 rope_theta = 500000.0
@@ -75,10 +77,12 @@
     return jnp.sum(jnp.where(same, row, 0.0), axis=1, keepdims=True)
 
 
-def fetch(pairs, sems):
+def fetch(pairs, sems, meanwhile=None):
     copies = [pltpu.make_async_copy(a, b, sems.at[at]) for at, (a, b) in enumerate(pairs)]
     for copy in copies:
         copy.start()
+    if meanwhile is not None:
+        meanwhile()
     for copy in copies:
         copy.wait()
 
@@ -137,9 +141,35 @@
     )(here, *in_hbm(inputs))
 
 
-def side_kernel(here_ref, *refs):
-    inputs, (out_ref, kpos_ref), scratch, sems = refs[:6], refs[6:8], refs[8:14], refs[14]
-    fetch(list(zip(inputs, scratch)), sems)
+def weight_parts(w_ref, pieces, refs, owners):
+    own_width = w_ref.shape[1] // owners
+    parts = []
+    for (first, last, start, width), ref in zip(pieces, refs):
+        for owner in range(owners):
+            columns = pl.ds(owner * own_width + start, width)
+            parts.append(
+                (w_ref.at[first:last, columns], ref.at[:, pl.ds(owner * width, width)])
+            )
+    return parts
+
+
+def weight_shapes(pieces, owners):
+    return [shape((last - first, owners * width)) for first, last, _, width in pieces]
+
+
+def side_kernel(pieces, owners, here_ref, w_ref, *refs):
+    inputs, outs, refs = refs[:6], refs[6:8], refs[8:]
+    held, scratch, sems, weight_sems = refs[: len(pieces)], refs[len(pieces) : -2], refs[-2], refs[-1]
+
+    def compute():
+        fetch(list(zip(inputs, scratch)), sems)
+        side_rows(here_ref, *scratch, *outs)
+
+    fetch(weight_parts(w_ref, pieces, held, owners), weight_sems, compute)
+
+
+def side_rows(here_ref, *refs):
+    (out_ref, kpos_ref), scratch = refs[-2:], refs[:-2]
     table_ref, source_ref, lengths_ref, offsets_ref, position_ref, q_ref = scratch
     count = q_ref.shape[0]
     cosine, sine = cos_sin(column(position_ref[...].astype(jnp.float32)), table_ref)
@@ -164,20 +194,22 @@
         )
 
 
-def side(here, source, lengths, offsets, positions, queries):
+def side(here, source, lengths, offsets, positions, queries, out_weight, pieces, owners):
     count, width = queries.shape
     tokens = source.shape[1] * PAGE
     inputs = (lane_tables(), source, lengths, offsets, positions, queries)
-    return pl.pallas_call(
-        side_kernel,
-        out_shape=(shape((count * (width // HD), HD)), shape((1, tokens), jnp.float32)),
-        in_specs=[SMEM] + [HBM] * 6,
-        out_specs=(VMEM, VMEM),
-        scratch_shapes=[vmem_like(x) for x in inputs] + [DMA((6,))],
+    outs = [shape((count * (width // HD), HD)), shape((1, tokens), jnp.float32)]
+    outs += weight_shapes(pieces, owners)
+    return pl.pallas_call(
+        lambda *refs: side_kernel(pieces, owners, *refs),
+        out_shape=outs,
+        in_specs=[SMEM] + [HBM] * 7,
+        out_specs=[VMEM] * len(outs),
+        scratch_shapes=[vmem_like(x) for x in inputs] + [DMA((6,)), DMA((len(pieces) * owners,))],
         name="side",
         compiler_params=params(6),
         cost_estimate=cost(8 * count * width, 64 * MIB),
-    )(here, *in_hbm(inputs))
+    )(here, *in_hbm((out_weight, *inputs)))
 
 
 def assemble_kernel(*refs):
@@ -277,7 +309,15 @@
     )(here, mine, other)
 
 
-def attention_kernel(*refs):
+def attention_kernel(pieces, owners, w_ref, *refs):
+    s_ref, sems = refs[-2:]
+    held = refs[-2 - len(pieces) : -2]
+    *refs, out_ref = refs[: -2 - len(pieces)]
+    parts = weight_parts(w_ref, pieces, held, owners)
+    fetch(parts, sems, lambda: attention_heads(*refs, out_ref, s_ref))
+
+
+def attention_heads(*refs):
     context, (q_ref, kpos_ref, qpos_ref, out_ref, s_ref) = refs[:-5], refs[-5:]
     count = qpos_ref.shape[1]
     heads = q_ref.shape[0] // count
@@ -322,25 +362,29 @@
         out_ref[:, pl.ds(pl.multiple_of(head * HD, HD), HD)] = (summed / total).astype(jnp.bfloat16)
         return carry
 
-    lax.fori_loop(0, heads, one, 0)
-
-
-def attend(context, q, key_positions, query_positions):
+    lax.fori_loop(0, heads, one, 0, unroll=UNROLL)
+
+
+def attend(context, q, key_positions, query_positions, out_weight, pieces, owners):
     tokens = key_positions.shape[1]
     count = query_positions.shape[1]
     heads = q.shape[0] // count
-    return pl.pallas_call(
-        attention_kernel,
-        out_shape=shape((count, heads * HD)),
-        in_specs=[VMEM] * (len(context) + 3),
-        out_specs=VMEM,
-        scratch_shapes=[pltpu.VMEM((count, tokens), jnp.float32)],
+    outs = [shape((count, heads * HD))] + weight_shapes(pieces, owners)
+    return pl.pallas_call(
+        lambda *refs: attention_kernel(pieces, owners, *refs),
+        out_shape=outs,
+        in_specs=[HBM] + [VMEM] * (len(context) + 3),
+        out_specs=[VMEM] * len(outs),
+        scratch_shapes=[
+            pltpu.VMEM((count, tokens), jnp.float32),
+            DMA((len(pieces) * owners,)),
+        ],
         name="attend",
         compiler_params=params(6),
         cost_estimate=cost(
             4 * count * heads * tokens * HD, 4 * tokens * HD, count * heads * tokens
         ),
-    )(*context, q, key_positions, query_positions)
+    )(*in_hbm([out_weight]), *context, q, key_positions, query_positions)
 
 
 def fold_masks(bits):
@@ -350,59 +394,67 @@
     return masks
 
 
-def columns_of(here_ref, mask, width, start, w_ref):
-    own_width = w_ref.shape[1] // (2 * KV)
-    first = jnp.bitwise_xor(here_ref[0], mask) * own_width + start
+def columns_of(here_ref, mask, width):
+    first = jnp.bitwise_xor(here_ref[0], mask) * width
     return pl.ds(pl.multiple_of(first, HD), width)
 
 
-def project_send_kernel(masks, start, here_ref, x_ref, w_ref, out_ref):
+def product(x_ref, w_refs, columns):
+    total, first = None, 0
+    for ref in w_refs:
+        last = first + ref.shape[0]
+        y = jnp.dot(x_ref[:, first:last], ref[:, columns], preferred_element_type=jnp.float32)
+        total = y if total is None else total + y
+        first = last
+    return total
+
+
+def project_send_kernel(masks, here_ref, x_ref, *refs):
+    *w_refs, out_ref = refs
     for at, mask in enumerate(masks):
-        columns = columns_of(here_ref, mask, out_ref.shape[2], start, w_ref)
-        out_ref[at] = jnp.dot(
-            x_ref[...], w_ref[:, columns], preferred_element_type=jnp.float32
-        ).astype(jnp.bfloat16)
-
-
-def project_keep_kernel(masks, start, here_ref, x_ref, w_ref, got_ref, send_ref, keep_ref):
+        columns = columns_of(here_ref, mask, out_ref.shape[2])
+        out_ref[at] = product(x_ref, w_refs, columns).astype(jnp.bfloat16)
+
+
+def project_keep_kernel(masks, here_ref, x_ref, *refs):
+    *w_refs, got_ref, send_ref, keep_ref = refs
     half = len(masks) // 2
     for at in list(range(half, 2 * half)) + list(range(half)):
-        columns = columns_of(here_ref, masks[at], got_ref.shape[2], start, w_ref)
-        y = jnp.dot(x_ref[...], w_ref[:, columns], preferred_element_type=jnp.float32)
-        y = y + got_ref[at].astype(jnp.float32)
+        columns = columns_of(here_ref, masks[at], got_ref.shape[2])
+        y = product(x_ref, w_refs, columns) + got_ref[at].astype(jnp.float32)
         if at >= half:
             send_ref[at - half] = y.astype(jnp.bfloat16)
         else:
             keep_ref[at] = y
 
 
-def project_cost(x, w, columns):
-    return cost(2 * x.shape[0] * w.shape[0] * columns, 2 * w.shape[0] * columns)
-
-
-def project_send(here, mixed, weight, masks, start, width):
+def project_cost(x, columns):
+    return cost(2 * x.shape[0] * x.shape[1] * columns, 2 * x.shape[1] * columns)
+
+
+def project_send(here, mixed, weights, masks, width):
     count = mixed.shape[0]
     return pl.pallas_call(
-        lambda *refs: project_send_kernel(masks, start, *refs),
+        lambda *refs: project_send_kernel(masks, *refs),
         out_shape=shape((len(masks), count, width)),
-        in_specs=[SMEM, VMEM, VMEM],
+        in_specs=[SMEM, VMEM] + [VMEM] * len(weights),
         out_specs=VMEM,
         compiler_params=params(6),
-        cost_estimate=project_cost(mixed, weight, len(masks) * width),
-    )(here, mixed, weight)
-
-
-def project_keep(here, mixed, weight, got, masks, start):
+        cost_estimate=project_cost(mixed, len(masks) * width),
+    )(here, mixed, *weights)
+
+
+def project_keep(here, mixed, weights, got, masks):
     count = mixed.shape[0]
     half, width = len(masks) // 2, got.shape[2]
     return pl.pallas_call(
-        lambda *refs: project_keep_kernel(masks, start, *refs),
+        lambda *refs: project_keep_kernel(masks, *refs),
         out_shape=(shape((half, count, width)), shape((half, count, width), jnp.float32)),
-        in_specs=[SMEM, VMEM, VMEM, VMEM],
+        in_specs=[SMEM, VMEM] + [VMEM] * len(weights) + [VMEM],
         out_specs=(VMEM, VMEM),
         compiler_params=params(6),
-        cost_estimate=project_cost(mixed, weight, len(masks) * width),
-    )(here, mixed, weight, got)
+        cost_estimate=project_cost(mixed, len(masks) * width),
+    )(here, mixed, *weights, got)
 
 
 def fold_kernel(keep_ref, got_ref, send_ref, left_ref):
@@ -469,16 +521,16 @@
     ]
 
 
-def project_and_scatter(here, devices, x, weight, chunks):
+def project_and_scatter(here, devices, x, weights, chunks):
     masks = [fold_masks(order) for _, _, order in chunks]
     half = devices // 2
     state, got = [], []
     for at, (start, width, order) in enumerate(chunks):
-        out = project_send(here, x, weight, masks[at][half:], start, width)
+        out = project_send(here, x, weights[at], masks[at][half:], width)
         got.append(swap(out, order[0], devices))
         x = after(x, out)
     for at, (start, _, _) in enumerate(chunks):
-        send, keep = project_keep(here, x, weight, got[at], masks[at][:half], start)
+        send, keep = project_keep(here, x, weights[at], got[at], masks[at][:half])
         state.append((send, keep))
         x = after(x, send)
     stages = len(chunks[0][2])
@@ -510,15 +562,26 @@
     )
     far = range(KV // 2, KV)
     arrived = [pieces[0]] + [swap(pieces[k], 2 * k, devices) for k in range(1, KV)]
-    turned, key_positions = side(here, source, lengths, offsets, positions, queries)
+    depth = out_weight.shape[0]
     chunks = plan(devices, out_weight.shape[1] // devices)
+    (start, width, _), (later, later_width, _) = chunks
+    early_rows = depth * EARLY // 16
+    early = [(0, early_rows, later, later_width)]
+    late = [(0, depth, start, width)]
+    if early_rows < depth:
+        late.append((early_rows, depth, later, later_width))
+    turned, key_positions, *early_weights = side(
+        here, source, lengths, offsets, positions, queries, out_weight, early, devices
+    )
     near = assemble(arrived[: KV // 2])
     far = assemble(arrived[KV // 2 :])
     context = [near, far, swap(near, 1, devices), swap(far, 1, devices)]
     leaving = order_pages(here, page_source, context)
     pages = [leaving[0]] + [swap(leaving[k], 2 * k, devices) for k in range(1, KV)]
-    mixed = attend(context, turned, key_positions, positions)
-    output = project_and_scatter(here, devices, mixed, out_weight, chunks)
+    mixed, *late_weights = attend(
+        context, turned, key_positions, positions, out_weight, late, devices
+    )
+    output = project_and_scatter(here, devices, mixed, [late_weights[:1], early_weights + late_weights[1:]], chunks)
     mine, partner = collect_heads(here, pages)
     new_keys, new_values = settle(here, mine, swap(partner, 1, devices))
     return (new_keys, new_values, output)

time: 94.9 us -> 89.7 us (0.945)
  local copies, waits for them, and re-layouts: 11.2 us -> 0.01 us
  Pallas kernels: 17.7 us -> 22.7 us
  waiting for transfers between devices: 30.8 us -> 31.9 us
    unnamed x6 -> x4, local copies, waits for them, and re-layouts: 11.2 us -> 0.01 us
    pallas_call x6, Pallas kernels: 13 us -> 18.1 us  [the longest x1 7.37 us: attend(): pl.pallas_call(lambda *refs: attention_kernel(pieces, owners, *refs), out...]
    ppermute x25, waiting for transfers between devices: 30.8 us -> 31.9 us  [swap(): return lax.ppermute(x, 'ctx', [(d, d ^ bits) for d in range(devices)])]
  transfers between devices with their start and end apart: 25 -> 25, of which waited for: 9 -> 11; matrix products, arithmetic and copies ran while one was open for 0% -> 0% of each run, Pallas kernels for 8% -> 12%
where the time goes in v2:
time: 89.7 us; the launch traced here: 89.5 us
  starting transfers between devices  34 us (38%)
  waiting for transfers between devices  31.9 us (36%)
  Pallas kernels  22.7 us (25%)
    ppermute x25, starting transfers between devices, swap(): return lax.ppermute(x, 'ctx', [(d, d ^ bits) for d in range(devices)])  34 us
    ppermute x25, waiting for transfers between devices, swap(): return lax.ppermute(x, 'ctx', [(d, d ^ bits) for d in range(devices)])  31.9 us
    pallas_call x1, Pallas kernels, attend(): pl.pallas_call(lambda *refs: attention_kernel(pieces, owners, *refs), out...  7.37 us
    pallas_call x1, Pallas kernels, side(): pl.pallas_call(lambda *refs: side_kernel(pieces, owners, *refs), out_shap...  5.5 us
    pallas_call x2, Pallas kernels, project_send(): pl.pallas_call(lambda *refs: project_send_kernel(masks, *refs), out_shape...  2.62 us
    pallas_call x2, Pallas kernels, project_keep(): pl.pallas_call(lambda *refs: project_keep_kernel(masks, *refs), out_shape...  2.58 us
  transfers between devices with their start and end apart: 25, of which 11 were waited for; matrix products, arithmetic and copies ran while one was open for 0% of the time, Pallas kernels for 12%

profile of v2, /device:TPU:0, one launch (start us, length us, event | category | flops | bytes accessed | tf_op | source)
XLA Modules:
  0.0 89.5 jit_solution(5769601397277567642)
XLA Ops:
  0.6 1.7 %prepare_rows.1 = (bf16[2,128,128]{2,1,0:T(8,128)(2,1)S(1)}, bf16[2,128,128]{2,1,0:T(8,128)(2,1)S(1)}, bf16[2,128,128]{2,1,0:T(8,128)(2,1)S(1)}, bf16[2,128,128]...) custom-call(s32[1]{0:T(128)} %bitcast.here_ref.refs_0_, ...), custom_call_target="tpu_custom_call" | custom-call | flops 2621440 | bytes 1048576 | tf_op jit(solution)/shard_map/prepare_rows/pallas_call | solution.py:132
  2.4 4.1 %collective-permute-start.3 = (bf16[2,128,128]{2,1,0:T(8,128)(2,1)S(1)}, bf16[2,128,128]{2,1,0:T(8,128)(2,1)S(1)}, u32[]{:S(2)}, u32[]{:S(2)}) collective-permute-start(bf16[2,128,128]{2,1,0:T(8,128)(2,1)S(1)} %get-tuple-element.48), channel_id=1, source_target_pairs={{0,8},{1,9},{2,10},{3,11},{4,12},{5,13},{6,14},{7,15},{8,0},{9,1},... | collective-permute-start | bytes 196616 | tf_op jit(solution)/shard_map/ppermute | solution.py:508
  6.5 1.3 %collective-permute-start.4 = (bf16[2,128,128]{2,1,0:T(8,128)(2,1)S(1)}, bf16[2,128,128]{2,1,0:T(8,128)(2,1)S(1)}, u32[]{:S(2)}, u32[]{:S(2)}) collective-permute-start(bf16[2,128,128]{2,1,0:T(8,128)(2,1)S(1)} %get-tuple-element.49), channel_id=1, source_target_pairs={{0,10},{1,11},{2,8},{3,9},{4,14},{5,15},{6,12},{7,13},{8,2},{9,3},... | collective-permute-start | bytes 196616 | tf_op jit(solution)/shard_map/ppermute | solution.py:508
  8.0 3.9 %collective-permute-start.5 = (bf16[2,128,128]{2,1,0:T(8,128)(2,1)S(1)}, bf16[2,128,128]{2,1,0:T(8,128)(2,1)S(1)}, u32[]{:S(2)}, u32[]{:S(2)}) collective-permute-start(bf16[2,128,128]{2,1,0:T(8,128)(2,1)S(1)} %get-tuple-element.50), channel_id=1, source_target_pairs={{0,12},{1,13},{2,14},{3,15},{4,8},{5,9},{6,10},{7,11},{8,4},{9,5},... | collective-permute-start | bytes 196616 | tf_op jit(solution)/shard_map/ppermute | solution.py:508
  11.9 1.2 %collective-permute-start.6 = (bf16[2,128,128]{2,1,0:T(8,128)(2,1)S(1)}, bf16[2,128,128]{2,1,0:T(8,128)(2,1)S(1)}, u32[]{:S(2)}, u32[]{:S(2)}) collective-permute-start(bf16[2,128,128]{2,1,0:T(8,128)(2,1)S(1)} %get-tuple-element.51), channel_id=1, source_target_pairs={{0,14},{1,15},{2,12},{3,13},{4,10},{5,11},{6,8},{7,9},{8,6},{9,7},... | collective-permute-start | bytes 196616 | tf_op jit(solution)/shard_map/ppermute | solution.py:508
  13.1 2.7 %collective-permute-done.4.refs_1_ = bf16[2,128,128]{2,1,0:T(8,128)(2,1)S(1)} collective-permute-done((bf16[2,128,128]{2,1,0:T(8,128)(2,1)S(1)}, bf16[2,128,128]{2,1,0:T(8,128)(2,1)S(1)}, u32[]{:S(2)}, u32[]{:S(2)}) %collective-permute-start.4) | collective-permute-done | bytes 65568 | tf_op jit(solution)/shard_map/ppermute | solution.py:508
  15.8 1.5 %collective-permute-start.2 = (bf16[2,128,128]{2,1,0:T(8,128)(2,1)S(1)}, bf16[2,128,128]{2,1,0:T(8,128)(2,1)S(1)}, u32[]{:S(2)}, u32[]{:S(2)}) collective-permute-start(bf16[2,128,128]{2,1,0:T(8,128)(2,1)S(1)} %get-tuple-element.47), channel_id=1, source_target_pairs={{0,6},{1,7},{2,4},{3,5},{4,2},{5,3},{6,0},{7,1},{8,14},{9,15},{10,... | collective-permute-start | bytes 196616 | tf_op jit(solution)/shard_map/ppermute | solution.py:508
  17.3 1.7 %collective-permute-done.6.refs_3_ = bf16[2,128,128]{2,1,0:T(8,128)(2,1)S(1)} collective-permute-done((bf16[2,128,128]{2,1,0:T(8,128)(2,1)S(1)}, bf16[2,128,128]{2,1,0:T(8,128)(2,1)S(1)}, u32[]{:S(2)}, u32[]{:S(2)}) %collective-permute-start.6) | collective-permute-done | bytes 65568 | tf_op jit(solution)/shard_map/ppermute | solution.py:508
  19.1 1.9 %collective-permute-done.2.refs_3_ = bf16[2,128,128]{2,1,0:T(8,128)(2,1)S(1)} collective-permute-done((bf16[2,128,128]{2,1,0:T(8,128)(2,1)S(1)}, bf16[2,128,128]{2,1,0:T(8,128)(2,1)S(1)}, u32[]{:S(2)}, u32[]{:S(2)}) %collective-permute-start.2) | collective-permute-done | bytes 65568 | tf_op jit(solution)/shard_map/ppermute | solution.py:508
  21.1 5.5 %side.1 = (bf16[1024,128]{1,0:T(8,128)(2,1)S(1)}, f32[1,2048]{1,0:T(1,128)S(1)}, bf16[768,8192]{1,0:T(8,128)(2,1)S(1)}) custom-call(s32[1]{0:T(128)} %bitcast.here_ref.refs_0_, bf16[1024,16384]{1,0:T(8,128)(2,1)} %refs_0_.3, f32[2,128]{1,0:T(2,128)} %constant.6.clone.refs_2_, s32[1,128]{1,0:T(1,128)} %bitcast.6, s32[1,128]{1,0:T(1,128)} %bitcast.10, ...), custom_call_target="tpu_custom_call" | custom-call | flops 1048576 | bytes 67108864 | tf_op jit(solution)/shard_map/side/pallas_call | solution.py:203
  26.6 7.4 %attend.1 = (bf16[128,1024]{1,0:T(8,128)(2,1)S(1)}, bf16[1024,8192]{1,0:T(8,128)(2,1)S(1)}, bf16[256,8192]{1,0:T(8,128)(2,1)S(1)}) custom-call(bf16[1024,16384]{1,0:T(8,128)(2,1)} %refs_0_.3, bf16[4,2,128,128]{3,2,1,0:T(8,128)(2,1)S(1)} %shard_map.139.refs_0_.refs_1_, bf16[4,2,128,128]{3,2,1,0:T(8,128)(2,1)S(1)} %shard_map.140.refs_1_.refs_2_, ...), custom_call_target="tpu_custom_call" | custom-call | flops 1073741824 | bytes 1048576 | tf_op jit(solution)/shard_map/attend/pallas_call | solution.py:373
  34.0 1.3 %shard_map.141 = bf16[8,128,512]{2,1,0:T(8,128)(2,1)S(1)} custom-call(s32[1]{0:T(128)} %bitcast.here_ref.refs_0_, bf16[128,1024]{1,0:T(8,128)(2,1)S(1)} %get-tuple-element.78.refs_1_, bf16[1024,8192]{1,0:T(8,128)(2,1)S(1)} %get-tuple-element.67.refs_2_), custom_call_target="tpu_custom_call" | custom-call | flops 1073741824 | bytes 8388608 | tf_op jit(solution)/shard_map/pallas_call | solution.py:437
  35.8 1.3 %shard_map.142 = bf16[8,128,512]{2,1,0:T(8,128)(2,1)S(1)} custom-call(s32[1]{0:T(128)} %bitcast.here_ref.refs_0_, bf16[128,1024]{1,0:T(8,128)(2,1)S(1)} %get-tuple-element.78.refs_1_, bf16[768,8192]{1,0:T(8,128)(2,1)S(1)} %get-tuple-element.69.refs_2_, bf16[256,8192]{1,0:T(8,128)(2,1)S(1)} %get-tuple-element.70.refs_3_), custom_call_target="tpu_custom_call" | custom-call | flops 1073741824 | bytes 8388608 | tf_op jit(solution)/shard_map/pallas_call | solution.py:437
  37.2 0.9 collective-permute-done.17.refs_3_
  38.1 1.3 %shard_map.143 = (bf16[4,128,512]{2,1,0:T(8,128)(2,1)S(1)}, f32[4,128,512]{2,1,0:T(8,128)S(1)}) custom-call(s32[1]{0:T(128)} %bitcast.here_ref.refs_0_, bf16[128,1024]{1,0:T(8,128)(2,1)S(1)} %get-tuple-element.78.refs_1_, bf16[1024,8192]{1,0:T(8,128)(2,1)S(1)} %get-tuple-element.67.refs_2_, bf16[8,128,512]{2,1,0:T(8,128)(2,1)S(1)} %collective-permute-done.17.refs_3_), custom_call_target="tpu_custom_call" | custom-call | flops 1073741824 | bytes 8388608 | tf_op jit(solution)/shard_map/pallas_call | solution.py:450
  39.9 1.3 %shard_map.146 = (bf16[4,128,512]{2,1,0:T(8,128)(2,1)S(1)}, f32[4,128,512]{2,1,0:T(8,128)S(1)}) custom-call(s32[1]{0:T(128)} %bitcast.here_ref.refs_0_, bf16[128,1024]{1,0:T(8,128)(2,1)S(1)} %get-tuple-element.78.refs_1_, bf16[768,8192]{1,0:T(8,128)(2,1)S(1)} %get-tuple-element.69.refs_2_, bf16[256,8192]{1,0:T(8,128)(2,1)S(1)} %get-tuple-element.70.refs_3_, ...), custom_call_target="tpu_custom_call" | custom-call | flops 1073741824 | bytes 8388608 | tf_op jit(solution)/shard_map/pallas_call | solution.py:450
  41.3 2.0 %collective-permute-start.18 = (bf16[4,128,512]{2,1,0:T(8,128)(2,1)S(1)}, bf16[4,128,512]{2,1,0:T(8,128)(2,1)S(1)}, u32[]{:S(2)}, u32[]{:S(2)}) collective-permute-start(bf16[4,128,512]{2,1,0:T(8,128)(2,1)S(1)} %get-tuple-element.73), channel_id=1, source_target_pairs={{0,2},{1,3},{2,0},{3,1},{4,6},{5,7},{6,4},{7,5},{8,10},{9,11},{10,... | collective-permute-start | bytes 1572872 | tf_op jit(solution)/shard_map/ppermute | solution.py:508
  43.3 0.9 order_pages.1
  44.3 1.9 %collective-permute-start.10 = (bf16[16,16,128]{2,1,0:T(8,128)(2,1)S(1)}, bf16[16,16,128]{2,1,0:T(8,128)(2,1)S(1)}, u32[]{:S(2)}, u32[]{:S(2)}) collective-permute-start(bf16[16,16,128]{2,1,0:T(8,128)(2,1)S(1)} %get-tuple-element.54), channel_id=1, source_target_pairs={{0,4},{1,5},{2,6},{3,7},{4,0},{5,1},{6,2},{7,3},{8,12},{9,13},{10,... | collective-permute-start | bytes 196616 | tf_op jit(solution)/shard_map/ppermute | solution.py:508
  46.2 1.5 %collective-permute-start.11 = (bf16[16,16,128]{2,1,0:T(8,128)(2,1)S(1)}, bf16[16,16,128]{2,1,0:T(8,128)(2,1)S(1)}, u32[]{:S(2)}, u32[]{:S(2)}) collective-permute-start(bf16[16,16,128]{2,1,0:T(8,128)(2,1)S(1)} %get-tuple-element.55), channel_id=1, source_target_pairs={{0,6},{1,7},{2,4},{3,5},{4,2},{5,3},{6,0},{7,1},{8,14},{9,15},{10,... | collective-permute-start | bytes 196616 | tf_op jit(solution)/shard_map/ppermute | solution.py:508
  47.8 8.3 %collective-permute-done.22.got_ref = bf16[4,128,512]{2,1,0:T(8,128)(2,1)S(1)} collective-permute-done((bf16[4,128,512]{2,1,0:T(8,128)(2,1)S(1)}, bf16[4,128,512]{2,1,0:T(8,128)(2,1)S(1)}, u32[]{:S(2)}, u32[]{:S(2)}) %collective-permute-start.22) | collective-permute-done | bytes 524320 | tf_op jit(solution)/shard_map/ppermute | solution.py:508
  56.0 2.9 %collective-permute-start.12 = (bf16[16,16,128]{2,1,0:T(8,128)(2,1)S(1)}, bf16[16,16,128]{2,1,0:T(8,128)(2,1)S(1)}, u32[]{:S(2)}, u32[]{:S(2)}) collective-permute-start(bf16[16,16,128]{2,1,0:T(8,128)(2,1)S(1)} %get-tuple-element.56), channel_id=1, source_target_pairs={{0,8},{1,9},{2,10},{3,11},{4,12},{5,13},{6,14},{7,15},{8,0},{9,1},... | collective-permute-start | bytes 196616 | tf_op jit(solution)/shard_map/ppermute | solution.py:508
  60.1 2.1 %collective-permute-start.19 = (bf16[2,128,512]{2,1,0:T(8,128)(2,1)S(1)}, bf16[2,128,512]{2,1,0:T(8,128)(2,1)S(1)}, u32[]{:S(2)}, u32[]{:S(2)}) collective-permute-start(bf16[2,128,512]{2,1,0:T(8,128)(2,1)S(1)} %get-tuple-element.75), channel_id=1, source_target_pairs={{0,4},{1,5},{2,6},{3,7},{4,0},{5,1},{6,2},{7,3},{8,12},{9,13},{10,... | collective-permute-start | bytes 786440 | tf_op jit(solution)/shard_map/ppermute | solution.py:508
  62.1 2.0 %collective-permute-start.13 = (bf16[16,16,128]{2,1,0:T(8,128)(2,1)S(1)}, bf16[16,16,128]{2,1,0:T(8,128)(2,1)S(1)}, u32[]{:S(2)}, u32[]{:S(2)}) collective-permute-start(bf16[16,16,128]{2,1,0:T(8,128)(2,1)S(1)} %get-tuple-element.57), channel_id=1, source_target_pairs={{0,10},{1,11},{2,8},{3,9},{4,14},{5,15},{6,12},{7,13},{8,2},{9,3},... | collective-permute-start | bytes 196616 | tf_op jit(solution)/shard_map/ppermute | solution.py:508
  64.1 1.2 %collective-permute-start.14 = (bf16[16,16,128]{2,1,0:T(8,128)(2,1)S(1)}, bf16[16,16,128]{2,1,0:T(8,128)(2,1)S(1)}, u32[]{:S(2)}, u32[]{:S(2)}) collective-permute-start(bf16[16,16,128]{2,1,0:T(8,128)(2,1)S(1)} %get-tuple-element.58), channel_id=1, source_target_pairs={{0,12},{1,13},{2,14},{3,15},{4,8},{5,9},{6,10},{7,11},{8,4},{9,5},... | collective-permute-start | bytes 196616 | tf_op jit(solution)/shard_map/ppermute | solution.py:508
  65.3 3.2 %collective-permute-start.15 = (bf16[16,16,128]{2,1,0:T(8,128)(2,1)S(1)}, bf16[16,16,128]{2,1,0:T(8,128)(2,1)S(1)}, u32[]{:S(2)}, u32[]{:S(2)}) collective-permute-start(bf16[16,16,128]{2,1,0:T(8,128)(2,1)S(1)} %get-tuple-element.59), channel_id=1, source_target_pairs={{0,14},{1,15},{2,12},{3,13},{4,10},{5,11},{6,8},{7,9},{8,6},{9,7},... | collective-permute-start | bytes 196616 | tf_op jit(solution)/shard_map/ppermute | solution.py:508
  68.5 1.3 %collective-permute-done.13.refs_5_ = bf16[16,16,128]{2,1,0:T(8,128)(2,1)S(1)} collective-permute-done((bf16[16,16,128]{2,1,0:T(8,128)(2,1)S(1)}, bf16[16,16,128]{2,1,0:T(8,128)(2,1)S(1)}, u32[]{:S(2)}, u32[]{:S(2)}) %collective-permute-start.13) | collective-permute-done | bytes 65568 | tf_op jit(solution)/shard_map/ppermute | solution.py:508
  69.8 3.1 %collective-permute-done.14.refs_6_ = bf16[16,16,128]{2,1,0:T(8,128)(2,1)S(1)} collective-permute-done((bf16[16,16,128]{2,1,0:T(8,128)(2,1)S(1)}, bf16[16,16,128]{2,1,0:T(8,128)(2,1)S(1)}, u32[]{:S(2)}, u32[]{:S(2)}) %collective-permute-start.14) | collective-permute-done | bytes 65568 | tf_op jit(solution)/shard_map/ppermute | solution.py:508
  73.5 1.7 %collective-permute-start.24 = (bf16[1,128,512]{2,1,0:T(8,128)(2,1)S(1)}, bf16[1,128,512]{2,1,0:T(8,128)(2,1)S(1)}, u32[]{:S(2)}, u32[]{:S(2)}) collective-permute-start(bf16[1,128,512]{2,1,0:T(8,128)(2,1)S(1)} %get-tuple-element.84), channel_id=1, source_target_pairs={{0,8},{1,9},{2,10},{3,11},{4,12},{5,13},{6,14},{7,15},{8,0},{9,1},... | collective-permute-start | bytes 393224 | tf_op jit(solution)/shard_map/ppermute | solution.py:508
  75.3 1.3 %collective-permute-start.20 = (bf16[1,128,512]{2,1,0:T(8,128)(2,1)S(1)}, bf16[1,128,512]{2,1,0:T(8,128)(2,1)S(1)}, u32[]{:S(2)}, u32[]{:S(2)}) collective-permute-start(bf16[1,128,512]{2,1,0:T(8,128)(2,1)S(1)} %get-tuple-element.77), channel_id=1, source_target_pairs={{0,8},{1,9},{2,10},{3,11},{4,12},{5,13},{6,14},{7,15},{8,0},{9,1},... | collective-permute-start | bytes 393224 | tf_op jit(solution)/shard_map/ppermute | solution.py:508
  77.4 8.8 %collective-permute-done.24.refs_3_ = bf16[1,128,512]{2,1,0:T(8,128)(2,1)S(1)} collective-permute-done((bf16[1,128,512]{2,1,0:T(8,128)(2,1)S(1)}, bf16[1,128,512]{2,1,0:T(8,128)(2,1)S(1)}, u32[]{:S(2)}, u32[]{:S(2)}) %collective-permute-start.24) | collective-permute-done | bytes 131104 | tf_op jit(solution)/shard_map/ppermute | solution.py:508
  86.3 2.5 %collective-permute-done.20.refs_1_ = bf16[1,128,512]{2,1,0:T(8,128)(2,1)S(1)} collective-permute-done((bf16[1,128,512]{2,1,0:T(8,128)(2,1)S(1)}, bf16[1,128,512]{2,1,0:T(8,128)(2,1)S(1)}, u32[]{:S(2)}, u32[]{:S(2)}) %collective-permute-start.20) | collective-permute-done | bytes 131104 | tf_op jit(solution)/shard_map/ppermute | solution.py:508
  (39 shorter events, 5.0 us)
Async XLA Ops:
  2.4 10.7 %collective-permute-start.3 = (bf16[2,128,128]{2,1,0:T(8,128)(2,1)S(1)}, bf16[2,128,128]{2,1,0:T(8,128)(2,1)S(1)}, u32[]{:S(2)}, u32[]{:S(2)}) collective-permute-start(bf16[2,128,128]{2,1,0:T(8,128)(2,1)S(1)} %get-tuple-element.48), channel_id=1, source_target_pairs={{0,8},{1,9},{2,10},{3,11},{4,12},{5,13},{6,14},{7,15},{8,0},{9,1},... | collective-permute-start | bytes 196616 | tf_op jit(solution)/shard_map/ppermute | solution.py:508
  6.5 9.3 %collective-permute-start.4 = (bf16[2,128,128]{2,1,0:T(8,128)(2,1)S(1)}, bf16[2,128,128]{2,1,0:T(8,128)(2,1)S(1)}, u32[]{:S(2)}, u32[]{:S(2)}) collective-permute-start(bf16[2,128,128]{2,1,0:T(8,128)(2,1)S(1)} %get-tuple-element.49), channel_id=1, source_target_pairs={{0,10},{1,11},{2,8},{3,9},{4,14},{5,15},{6,12},{7,13},{8,2},{9,3},... | collective-permute-start | bytes 196616 | tf_op jit(solution)/shard_map/ppermute | solution.py:508
  7.8 11.3 %collective-permute-start = (bf16[2,128,128]{2,1,0:T(8,128)(2,1)S(1)}, bf16[2,128,128]{2,1,0:T(8,128)(2,1)S(1)}, u32[]{:S(2)}, u32[]{:S(2)}) collective-permute-start(bf16[2,128,128]{2,1,0:T(8,128)(2,1)S(1)} %get-tuple-element.45), channel_id=1, source_target_pairs={{0,2},{1,3},{2,0},{3,1},{4,6},{5,7},{6,4},{7,5},{8,10},{9,11},{10,... | collective-permute-start | bytes 196616 | tf_op jit(solution)/shard_map/ppermute | solution.py:508
  8.0 9.3 %collective-permute-start.5 = (bf16[2,128,128]{2,1,0:T(8,128)(2,1)S(1)}, bf16[2,128,128]{2,1,0:T(8,128)(2,1)S(1)}, u32[]{:S(2)}, u32[]{:S(2)}) collective-permute-start(bf16[2,128,128]{2,1,0:T(8,128)(2,1)S(1)} %get-tuple-element.50), channel_id=1, source_target_pairs={{0,12},{1,13},{2,14},{3,15},{4,8},{5,9},{6,10},{7,11},{8,4},{9,5},... | collective-permute-start | bytes 196616 | tf_op jit(solution)/shard_map/ppermute | solution.py:508
  11.9 7.1 %collective-permute-start.6 = (bf16[2,128,128]{2,1,0:T(8,128)(2,1)S(1)}, bf16[2,128,128]{2,1,0:T(8,128)(2,1)S(1)}, u32[]{:S(2)}, u32[]{:S(2)}) collective-permute-start(bf16[2,128,128]{2,1,0:T(8,128)(2,1)S(1)} %get-tuple-element.51), channel_id=1, source_target_pairs={{0,14},{1,15},{2,12},{3,13},{4,10},{5,11},{6,8},{7,9},{8,6},{9,7},... | collective-permute-start | bytes 196616 | tf_op jit(solution)/shard_map/ppermute | solution.py:508
  13.1 6.0 %collective-permute-start.1 = (bf16[2,128,128]{2,1,0:T(8,128)(2,1)S(1)}, bf16[2,128,128]{2,1,0:T(8,128)(2,1)S(1)}, u32[]{:S(2)}, u32[]{:S(2)}) collective-permute-start(bf16[2,128,128]{2,1,0:T(8,128)(2,1)S(1)} %get-tuple-element.46), channel_id=1, source_target_pairs={{0,4},{1,5},{2,6},{3,7},{4,0},{5,1},{6,2},{7,3},{8,12},{9,13},{10,... | collective-permute-start | bytes 196616 | tf_op jit(solution)/shard_map/ppermute | solution.py:508
  15.8 5.2 %collective-permute-start.2 = (bf16[2,128,128]{2,1,0:T(8,128)(2,1)S(1)}, bf16[2,128,128]{2,1,0:T(8,128)(2,1)S(1)}, u32[]{:S(2)}, u32[]{:S(2)}) collective-permute-start(bf16[2,128,128]{2,1,0:T(8,128)(2,1)S(1)} %get-tuple-element.47), channel_id=1, source_target_pairs={{0,6},{1,7},{2,4},{3,5},{4,2},{5,3},{6,0},{7,1},{8,14},{9,15},{10,... | collective-permute-start | bytes 196616 | tf_op jit(solution)/shard_map/ppermute | solution.py:508
  19.0 7.6 %collective-permute-start.8 = (bf16[4,2,128,128]{3,2,1,0:T(8,128)(2,1)S(1)}, bf16[4,2,128,128]{3,2,1,0:T(8,128)(2,1)S(1)}, u32[]{:S(2)}, u32[]{:S(2)}) collective-permute-start(bf16[4,2,128,128]{3,2,1,0:T(8,128)(2,1)S(1)} %shard_map.140.refs_1_.refs_2_), channel_id=1, source_target_pairs={{0,1},{1,0},{2,3},{3,2},{4,5},{5,4},{6,7},{7,6},{8,9},{9,8},{10,11... | collective-permute-start | bytes 786440 | tf_op jit(solution)/shard_map/ppermute | solution.py:508
  21.0 5.6 %collective-permute-start.7 = (bf16[4,2,128,128]{3,2,1,0:T(8,128)(2,1)S(1)}, bf16[4,2,128,128]{3,2,1,0:T(8,128)(2,1)S(1)}, u32[]{:S(2)}, u32[]{:S(2)}) collective-permute-start(bf16[4,2,128,128]{3,2,1,0:T(8,128)(2,1)S(1)} %shard_map.139.refs_0_.refs_1_), channel_id=1, source_target_pairs={{0,1},{1,0},{2,3},{3,2},{4,5},{5,4},{6,7},{7,6},{8,9},{9,8},{10,11... | collective-permute-start | bytes 786440 | tf_op jit(solution)/shard_map/ppermute | solution.py:508
  21.1 5.5 %copy-start.1 = (s32[128]{0:T(128)S(1)}, s32[128]{0:T(128)}, u32[]{:S(2)}) copy-start(s32[128]{0:T(128)} %param.19) | copy-start | bytes 1540
  35.3 2.8 %collective-permute-start.17 = (bf16[8,128,512]{2,1,0:T(8,128)(2,1)S(1)}, bf16[8,128,512]{2,1,0:T(8,128)(2,1)S(1)}, u32[]{:S(2)}, u32[]{:S(2)}) collective-permute-start(bf16[8,128,512]{2,1,0:T(8,128)(2,1)S(1)} %shard_map.141), channel_id=1, source_target_pairs={{0,1},{1,0},{2,3},{3,2},{4,5},{5,4},{6,7},{7,6},{8,9},{9,8},{10,11... | collective-permute-start | bytes 3145736 | tf_op jit(solution)/shard_map/ppermute | solution.py:508
  37.1 6.2 %copy-start = (s32[128]{0:T(128)S(1)}, s32[128]{0:T(128)}, u32[]{:S(2)}) copy-start(s32[128]{0:T(128)} %source_ref.1) | copy-start | bytes 1540
  37.2 2.7 %collective-permute-start.21 = (bf16[8,128,512]{2,1,0:T(8,128)(2,1)S(1)}, bf16[8,128,512]{2,1,0:T(8,128)(2,1)S(1)}, u32[]{:S(2)}, u32[]{:S(2)}) collective-permute-start(bf16[8,128,512]{2,1,0:T(8,128)(2,1)S(1)} %shard_map.142), channel_id=1, source_target_pairs={{0,1},{1,0},{2,3},{3,2},{4,5},{5,4},{6,7},{7,6},{8,9},{9,8},{10,11... | collective-permute-start | bytes 3145736 | tf_op jit(solution)/shard_map/ppermute | solution.py:508
  41.2 14.9 %collective-permute-start.22 = (bf16[4,128,512]{2,1,0:T(8,128)(2,1)S(1)}, bf16[4,128,512]{2,1,0:T(8,128)(2,1)S(1)}, u32[]{:S(2)}, u32[]{:S(2)}) collective-permute-start(bf16[4,128,512]{2,1,0:T(8,128)(2,1)S(1)} %get-tuple-element.80), channel_id=1, source_target_pairs={{0,4},{1,5},{2,6},{3,7},{4,0},{5,1},{6,2},{7,3},{8,12},{9,13},{10,... | collective-permute-start | bytes 1572872 | tf_op jit(solution)/shard_map/ppermute | solution.py:508
  41.3 17.8 %collective-permute-start.18 = (bf16[4,128,512]{2,1,0:T(8,128)(2,1)S(1)}, bf16[4,128,512]{2,1,0:T(8,128)(2,1)S(1)}, u32[]{:S(2)}, u32[]{:S(2)}) collective-permute-start(bf16[4,128,512]{2,1,0:T(8,128)(2,1)S(1)} %get-tuple-element.73), channel_id=1, source_target_pairs={{0,2},{1,3},{2,0},{3,1},{4,6},{5,7},{6,4},{7,5},{8,10},{9,11},{10,... | collective-permute-start | bytes 1572872 | tf_op jit(solution)/shard_map/ppermute | solution.py:508
  44.2 15.8 %collective-permute-start.9 = (bf16[16,16,128]{2,1,0:T(8,128)(2,1)S(1)}, bf16[16,16,128]{2,1,0:T(8,128)(2,1)S(1)}, u32[]{:S(2)}, u32[]{:S(2)}) collective-permute-start(bf16[16,16,128]{2,1,0:T(8,128)(2,1)S(1)} %get-tuple-element.53), channel_id=1, source_target_pairs={{0,2},{1,3},{2,0},{3,1},{4,6},{5,7},{6,4},{7,5},{8,10},{9,11},{10,... | collective-permute-start | bytes 196616 | tf_op jit(solution)/shard_map/ppermute | solution.py:508
  44.3 17.9 %collective-permute-start.10 = (bf16[16,16,128]{2,1,0:T(8,128)(2,1)S(1)}, bf16[16,16,128]{2,1,0:T(8,128)(2,1)S(1)}, u32[]{:S(2)}, u32[]{:S(2)}) collective-permute-start(bf16[16,16,128]{2,1,0:T(8,128)(2,1)S(1)} %get-tuple-element.54), channel_id=1, source_target_pairs={{0,4},{1,5},{2,6},{3,7},{4,0},{5,1},{6,2},{7,3},{8,12},{9,13},{10,... | collective-permute-start | bytes 196616 | tf_op jit(solution)/shard_map/ppermute | solution.py:508
  46.2 17.9 %collective-permute-start.11 = (bf16[16,16,128]{2,1,0:T(8,128)(2,1)S(1)}, bf16[16,16,128]{2,1,0:T(8,128)(2,1)S(1)}, u32[]{:S(2)}, u32[]{:S(2)}) collective-permute-start(bf16[16,16,128]{2,1,0:T(8,128)(2,1)S(1)} %get-tuple-element.55), channel_id=1, source_target_pairs={{0,6},{1,7},{2,4},{3,5},{4,2},{5,3},{6,0},{7,1},{8,14},{9,15},{10,... | collective-permute-start | bytes 196616 | tf_op jit(solution)/shard_map/ppermute | solution.py:508
  56.0 9.3 %collective-permute-start.12 = (bf16[16,16,128]{2,1,0:T(8,128)(2,1)S(1)}, bf16[16,16,128]{2,1,0:T(8,128)(2,1)S(1)}, u32[]{:S(2)}, u32[]{:S(2)}) collective-permute-start(bf16[16,16,128]{2,1,0:T(8,128)(2,1)S(1)} %get-tuple-element.56), channel_id=1, source_target_pairs={{0,8},{1,9},{2,10},{3,11},{4,12},{5,13},{6,14},{7,15},{8,0},{9,1},... | collective-permute-start | bytes 196616 | tf_op jit(solution)/shard_map/ppermute | solution.py:508
  59.1 14.3 %collective-permute-start.23 = (bf16[2,128,512]{2,1,0:T(8,128)(2,1)S(1)}, bf16[2,128,512]{2,1,0:T(8,128)(2,1)S(1)}, u32[]{:S(2)}, u32[]{:S(2)}) collective-permute-start(bf16[2,128,512]{2,1,0:T(8,128)(2,1)S(1)} %get-tuple-element.82), channel_id=1, source_target_pairs={{0,2},{1,3},{2,0},{3,1},{4,6},{5,7},{6,4},{7,5},{8,10},{9,11},{10,... | collective-permute-start | bytes 786440 | tf_op jit(solution)/shard_map/ppermute | solution.py:508
  60.1 15.2 %collective-permute-start.19 = (bf16[2,128,512]{2,1,0:T(8,128)(2,1)S(1)}, bf16[2,128,512]{2,1,0:T(8,128)(2,1)S(1)}, u32[]{:S(2)}, u32[]{:S(2)}) collective-permute-start(bf16[2,128,512]{2,1,0:T(8,128)(2,1)S(1)} %get-tuple-element.75), channel_id=1, source_target_pairs={{0,4},{1,5},{2,6},{3,7},{4,0},{5,1},{6,2},{7,3},{8,12},{9,13},{10,... | collective-permute-start | bytes 786440 | tf_op jit(solution)/shard_map/ppermute | solution.py:508
  62.1 7.7 %collective-permute-start.13 = (bf16[16,16,128]{2,1,0:T(8,128)(2,1)S(1)}, bf16[16,16,128]{2,1,0:T(8,128)(2,1)S(1)}, u32[]{:S(2)}, u32[]{:S(2)}) collective-permute-start(bf16[16,16,128]{2,1,0:T(8,128)(2,1)S(1)} %get-tuple-element.57), channel_id=1, source_target_pairs={{0,10},{1,11},{2,8},{3,9},{4,14},{5,15},{6,12},{7,13},{8,2},{9,3},... | collective-permute-start | bytes 196616 | tf_op jit(solution)/shard_map/ppermute | solution.py:508
  64.1 8.8 %collective-permute-start.14 = (bf16[16,16,128]{2,1,0:T(8,128)(2,1)S(1)}, bf16[16,16,128]{2,1,0:T(8,128)(2,1)S(1)}, u32[]{:S(2)}, u32[]{:S(2)}) collective-permute-start(bf16[16,16,128]{2,1,0:T(8,128)(2,1)S(1)} %get-tuple-element.58), channel_id=1, source_target_pairs={{0,12},{1,13},{2,14},{3,15},{4,8},{5,9},{6,10},{7,11},{8,4},{9,5},... | collective-permute-start | bytes 196616 | tf_op jit(solution)/shard_map/ppermute | solution.py:508
  65.3 7.9 %collective-permute-start.15 = (bf16[16,16,128]{2,1,0:T(8,128)(2,1)S(1)}, bf16[16,16,128]{2,1,0:T(8,128)(2,1)S(1)}, u32[]{:S(2)}, u32[]{:S(2)}) collective-permute-start(bf16[16,16,128]{2,1,0:T(8,128)(2,1)S(1)} %get-tuple-element.59), channel_id=1, source_target_pairs={{0,14},{1,15},{2,12},{3,13},{4,10},{5,11},{6,8},{7,9},{8,6},{9,7},... | collective-permute-start | bytes 196616 | tf_op jit(solution)/shard_map/ppermute | solution.py:508
  73.3 3.2 %collective-permute-start.16 = (bf16[128,1024]{1,0:T(8,128)(2,1)S(1)}, bf16[128,1024]{1,0:T(8,128)(2,1)S(1)}, u32[]{:S(2)}, u32[]{:S(2)}) collective-permute-start(bf16[128,1024]{1,0:T(8,128)(2,1)S(1)} %get-tuple-element.61), channel_id=1, source_target_pairs={{0,1},{1,0},{2,3},{3,2},{4,5},{5,4},{6,7},{7,6},{8,9},{9,8},{10,11... | collective-permute-start | bytes 786440 | tf_op jit(solution)/shard_map/ppermute | solution.py:508
  73.5 12.8 %collective-permute-start.24 = (bf16[1,128,512]{2,1,0:T(8,128)(2,1)S(1)}, bf16[1,128,512]{2,1,0:T(8,128)(2,1)S(1)}, u32[]{:S(2)}, u32[]{:S(2)}) collective-permute-start(bf16[1,128,512]{2,1,0:T(8,128)(2,1)S(1)} %get-tuple-element.84), channel_id=1, source_target_pairs={{0,8},{1,9},{2,10},{3,11},{4,12},{5,13},{6,14},{7,15},{8,0},{9,1},... | collective-permute-start | bytes 393224 | tf_op jit(solution)/shard_map/ppermute | solution.py:508
  75.3 13.5 %collective-permute-start.20 = (bf16[1,128,512]{2,1,0:T(8,128)(2,1)S(1)}, bf16[1,128,512]{2,1,0:T(8,128)(2,1)S(1)}, u32[]{:S(2)}, u32[]{:S(2)}) collective-permute-start(bf16[1,128,512]{2,1,0:T(8,128)(2,1)S(1)} %get-tuple-element.77), channel_id=1, source_target_pairs={{0,8},{1,9},{2,10},{3,11},{4,12},{5,13},{6,14},{7,15},{8,0},{9,1},... | collective-permute-start | bytes 393224 | tf_op jit(solution)/shard_map/ppermute | solution.py:508

commit v3 on v2

--- a/solution.py
+++ b/solution.py
@@ -14,8 +14,9 @@
 HD = 128
 PAGE = 16
 MIB = 1 << 20
-UNROLL = 1
-EARLY = 12
+BLOCK = 512
+HEADS_AT_ONCE = 2
+SHARE = 4
 
 
 rope_theta = 500000.0
@@ -95,8 +96,17 @@
     return pltpu.VMEM(x.shape, x.dtype)
 
 
-def rows_kernel(here_ref, *refs):
-    inputs, out_refs, scratch, sems = refs[:8], refs[8:-9], refs[-9:-1], refs[-1]
+def rows_kernel(pieces, owners, here_ref, w_ref, *refs):
+    inputs, outs, scratch = refs[:8], refs[8:-10], refs[-10:-2]
+    sems, weight_sems = refs[-2:]
+
+    def compute():
+        fetch_and_turn(here_ref, inputs, scratch, sems, outs[:KV])
+
+    fetch(weight_parts(w_ref, pieces, outs[KV:], owners), weight_sems, compute)
+
+
+def fetch_and_turn(here_ref, inputs, scratch, sems, out_refs):
     fetch(list(zip(inputs, scratch)), sems)
     ks_ref, vs_ref, table_ref, source_ref, lengths_ref, offsets_ref, pk_ref, pv_ref = scratch
     rows = pk_ref.shape[0]
@@ -124,21 +134,24 @@
             out_ref[1, part, :] = (v * live[part]).astype(jnp.bfloat16)
 
 
-def prepare_rows(here, pool_keys, pool_values, key_scales, value_scales, source, lengths, offsets):
+def prepare_rows(here, out_weight, pieces, owners, *tables):
+    pool_keys, pool_values, key_scales, value_scales, source, lengths, offsets = tables
     rows = pool_keys.shape[0]
     table = lane_tables()
     small = [pltpu.SMEM(key_scales.shape, jnp.float32)] * 2
     inputs = (key_scales, value_scales, table, source, lengths, offsets, pool_keys, pool_values)
-    return pl.pallas_call(
-        rows_kernel,
-        out_shape=[shape((2, rows, HD))] * KV,
-        in_specs=[SMEM] + [HBM] * 8,
-        out_specs=[VMEM] * KV,
-        scratch_shapes=small + [vmem_like(x) for x in inputs[2:]] + [DMA((8,))],
+    outs = [shape((2, rows, HD))] * KV + weight_shapes(pieces, owners)
+    sems = [DMA((8,)), DMA((max(1, len(pieces)) * owners,))]
+    return pl.pallas_call(
+        lambda *refs: rows_kernel(pieces, owners, *refs),
+        out_shape=outs,
+        in_specs=[SMEM] + [HBM] * 9,
+        out_specs=[VMEM] * len(outs),
+        scratch_shapes=small + [vmem_like(x) for x in inputs[2:]] + sems,
         name="prepare_rows",
         compiler_params=params(6),
         cost_estimate=cost(20 * rows * KV * HD, 8 * rows * KV * HD),
-    )(here, *in_hbm(inputs))
+    )(here, *in_hbm((out_weight, *inputs)))
 
 
 def weight_parts(w_ref, pieces, refs, owners):
@@ -230,7 +243,7 @@
 
 
 def pages_kernel(here_ref, source_ref, *refs):
-    context, out_refs, page_ref, place_ref = refs[: -KV - 2], refs[-KV - 2 : -2], refs[-2], refs[-1]
+    *context, near_ref, far_ref, page_ref, place_ref = refs
     pages = source_ref.shape[0]
     slots = pages // (2 * KV)
     here = here_ref[0]
@@ -246,18 +259,19 @@
                 page = place_ref[device * slots + slot]
                 page_ref[page] = ref[at, kind, slot * PAGE : (slot + 1) * PAGE, :]
             group += 1
-    for piece, out_ref in enumerate(out_refs):
+    for piece in range(KV):
         first = jnp.bitwise_xor(here // 2, piece) * 2 * slots
-        out_ref[...] = page_ref[pl.ds(first, 2 * slots)]
+        out_ref = near_ref if piece < KV // 2 else far_ref
+        out_ref[piece % (KV // 2)] = page_ref[pl.ds(first, 2 * slots)]
 
 
 def order_pages(here, source, context):
     pages = source.shape[0]
     return pl.pallas_call(
         pages_kernel,
-        out_shape=[shape((pages // KV, PAGE, HD))] * KV,
+        out_shape=[shape((KV // 2, pages // KV, PAGE, HD))] * 2,
         in_specs=[SMEM, SMEM] + [VMEM] * len(context),
-        out_specs=[VMEM] * KV,
+        out_specs=[VMEM] * 2,
         scratch_shapes=[pltpu.VMEM((pages, PAGE, HD), jnp.bfloat16), pltpu.SMEM((pages,), jnp.int32)],
         name="order_pages",
         compiler_params=params(4),
@@ -265,30 +279,67 @@
     )(here, source, *context)
 
 
-def collect_kernel(here_ref, *refs):
-    pieces, (keep_ref, send_ref) = refs[:-2], refs[-2:]
+def forward_kernel(first, *refs):
+    *held, out_ref = refs
+    at = 0
+    for ref in held:
+        for row in range(ref.shape[0]):
+            out_ref[at] = ref[row, first : first + out_ref.shape[1]]
+            at += 1
+
+
+def forward(held, first):
+    count = sum(x.shape[0] for x in held)
+    dims = (count, first, *held[0].shape[2:])
+    return pl.pallas_call(
+        lambda *refs: forward_kernel(first, *refs),
+        out_shape=shape(dims),
+        in_specs=[VMEM] * len(held),
+        out_specs=VMEM,
+        compiler_params=params(4),
+        cost_estimate=cost(0, 4 * math.prod(dims)),
+    )(*held)
+
+
+def send_pages(near, far, devices):
+    held, heads = [near[None]], [0]
+    send = far[None]
+    bit = KV // 2
+    while True:
+        held.append(swap(send, 2 * bit, devices))
+        heads += [head | bit for head in heads]
+        bit //= 2
+        if not bit:
+            break
+        send = forward(held, bit)
+    return held, heads
+
+
+def collect_kernel(heads, here_ref, *refs):
+    *held, keep_ref, send_ref = refs
     rows = keep_ref.shape[0]
     slots = rows // PAGE
     core = here_ref[0] % 2
-    for piece, ref in enumerate(pieces):
-        head = jnp.bitwise_xor(here_ref[0] // 2, piece)
+    pieces = [(ref, row) for ref in held for row in range(ref.shape[0])]
+    for (ref, row), apart in zip(pieces, heads):
+        head = jnp.bitwise_xor(here_ref[0] // 2, apart)
         lanes = pl.ds(pl.multiple_of(head * HD, HD), HD)
-        keep_ref[:, lanes] = ref[pl.ds(core * slots, slots)].reshape(rows, HD)
-        send_ref[:, lanes] = ref[pl.ds((1 - core) * slots, slots)].reshape(rows, HD)
-
-
-def collect_heads(here, pieces):
-    rows = pieces[0].shape[0] * PAGE // 2
+        keep_ref[:, lanes] = ref[row, 0, pl.ds(core * slots, slots)].reshape(rows, HD)
+        send_ref[:, lanes] = ref[row, 0, pl.ds((1 - core) * slots, slots)].reshape(rows, HD)
+
+
+def collect_heads(here, held, heads):
+    rows = held[0].shape[2] * PAGE // 2
     out = shape((rows, KV * HD))
     return pl.pallas_call(
-        collect_kernel,
+        lambda *refs: collect_kernel(heads, *refs),
         out_shape=(out, out),
-        in_specs=[SMEM] + [VMEM] * KV,
+        in_specs=[SMEM] + [VMEM] * len(held),
         out_specs=(VMEM, VMEM),
         name="collect_heads",
         compiler_params=params(4),
         cost_estimate=cost(0, 8 * rows * KV * HD),
-    )(here, *pieces)
+    )(here, *held)
 
 
 def settle_kernel(here_ref, mine_ref, other_ref, keys_ref, values_ref):
@@ -321,20 +372,23 @@
     context, (q_ref, kpos_ref, qpos_ref, out_ref, s_ref) = refs[:-5], refs[-5:]
     count = qpos_ref.shape[1]
     heads = q_ref.shape[0] // count
+    group = s_ref.shape[0] // count
     rows = context[0].shape[2]
     blocks, at = [], 0
     for ref in context:
-        step = max(1, min(ref.shape[0], 512 // rows))
+        step = max(1, min(ref.shape[0], BLOCK // rows))
         for first in range(0, ref.shape[0], step):
             blocks.append((ref, slice(first, first + step), slice(at, at + step * rows)))
             at += step * rows
     block = step * rows
     scale = HD**-0.5 * math.log2(math.e)
     qpos = column(qpos_ref[...].astype(jnp.float32))
-
-    def one(head, carry):
-        q = q_ref[pl.ds(pl.multiple_of(head * count, count), count), :]
-        top = jnp.full((count, HD), masked_score, jnp.float32)
+    qpos = jnp.concatenate([qpos] * group, axis=0)
+    size = group * count
+
+    def one(index, carry):
+        q = q_ref[pl.ds(pl.multiple_of(index * size, size), size), :]
+        top = jnp.full((size, HD), masked_score, jnp.float32)
         for ref, chips, lanes in blocks:
             s = lax.dot_general(
                 q,
@@ -347,8 +401,8 @@
             for lane in range(0, block, HD):
                 top = jnp.maximum(top, s[:, lane : lane + HD])
         top = jnp.max(top, axis=1, keepdims=True)
-        total = jnp.zeros((count, HD), jnp.float32)
-        summed = jnp.zeros((count, HD), jnp.float32)
+        total = jnp.zeros((size, HD), jnp.float32)
+        summed = jnp.zeros((size, HD), jnp.float32)
         for ref, chips, lanes in blocks:
             w = jnp.exp2((s_ref[:, lanes] - top) * scale)
             for lane in range(0, block, HD):
@@ -358,11 +412,13 @@
                 ref[chips, 1].reshape(block, HD),
                 preferred_element_type=jnp.float32,
             )
-        total = jnp.sum(total, axis=1, keepdims=True)
-        out_ref[:, pl.ds(pl.multiple_of(head * HD, HD), HD)] = (summed / total).astype(jnp.bfloat16)
+        out = (summed / jnp.sum(total, axis=1, keepdims=True)).astype(jnp.bfloat16)
+        for at in range(group):
+            lanes = pl.ds(pl.multiple_of((index * group + at) * HD, HD), HD)
+            out_ref[:, lanes] = out[at * count : (at + 1) * count]
         return carry
 
-    lax.fori_loop(0, heads, one, 0, unroll=UNROLL)
+    lax.fori_loop(0, heads // group, one, 0, unroll=2)
 
 
 def attend(context, q, key_positions, query_positions, out_weight, pieces, owners):
@@ -376,11 +432,11 @@
         in_specs=[HBM] + [VMEM] * (len(context) + 3),
         out_specs=[VMEM] * len(outs),
         scratch_shapes=[
-            pltpu.VMEM((count, tokens), jnp.float32),
+            pltpu.VMEM((math.gcd(heads, HEADS_AT_ONCE) * count, tokens), jnp.float32),
             DMA((len(pieces) * owners,)),
         ],
         name="attend",
-        compiler_params=params(6),
+        compiler_params=params(8),
         cost_estimate=cost(
             4 * count * heads * tokens * HD, 4 * tokens * HD, count * heads * tokens
         ),
@@ -409,49 +465,52 @@
     return total
 
 
-def project_send_kernel(masks, here_ref, x_ref, *refs):
-    *w_refs, out_ref = refs
+def project_send_kernel(masks, pieces, owners, here_ref, w_ref, x_ref, *refs):
+    held, sems = refs[len(refs) - 1 - len(pieces) : -1], refs[-1]
+    *w_refs, out_ref = refs[: len(refs) - 1 - len(pieces)]
+
+    def compute():
+        for at, mask in enumerate(masks):
+            columns = columns_of(here_ref, mask, out_ref.shape[2])
+            out_ref[at] = product(x_ref, w_refs, columns).astype(jnp.bfloat16)
+
+    fetch(weight_parts(w_ref, pieces, held, owners), sems, compute)
+
+
+def project_add_kernel(masks, first, here_ref, x_ref, *refs):
+    *w_refs, got_ref, out_ref = refs
     for at, mask in enumerate(masks):
-        columns = columns_of(here_ref, mask, out_ref.shape[2])
-        out_ref[at] = product(x_ref, w_refs, columns).astype(jnp.bfloat16)
-
-
-def project_keep_kernel(masks, here_ref, x_ref, *refs):
-    *w_refs, got_ref, send_ref, keep_ref = refs
-    half = len(masks) // 2
-    for at in list(range(half, 2 * half)) + list(range(half)):
-        columns = columns_of(here_ref, masks[at], got_ref.shape[2])
-        y = product(x_ref, w_refs, columns) + got_ref[at].astype(jnp.float32)
-        if at >= half:
-            send_ref[at - half] = y.astype(jnp.bfloat16)
-        else:
-            keep_ref[at] = y
+        columns = columns_of(here_ref, mask, got_ref.shape[2])
+        y = product(x_ref, w_refs, columns) + got_ref[first + at].astype(jnp.float32)
+        out_ref[at] = y.astype(out_ref.dtype)
 
 
 def project_cost(x, columns):
     return cost(2 * x.shape[0] * x.shape[1] * columns, 2 * x.shape[1] * columns)
 
 
-def project_send(here, mixed, weights, masks, width):
+def project_send(here, mixed, weights, masks, width, out_weight, pieces, owners):
     count = mixed.shape[0]
-    return pl.pallas_call(
-        lambda *refs: project_send_kernel(masks, *refs),
-        out_shape=shape((len(masks), count, width)),
-        in_specs=[SMEM, VMEM] + [VMEM] * len(weights),
-        out_specs=VMEM,
+    outs = [shape((len(masks), count, width))] + weight_shapes(pieces, owners)
+    return pl.pallas_call(
+        lambda *refs: project_send_kernel(masks, pieces, owners, *refs),
+        out_shape=outs,
+        in_specs=[SMEM, HBM, VMEM] + [VMEM] * len(weights),
+        out_specs=[VMEM] * len(outs),
+        scratch_shapes=[DMA((max(1, len(pieces)) * owners,))],
         compiler_params=params(6),
         cost_estimate=project_cost(mixed, len(masks) * width),
-    )(here, mixed, *weights)
-
-
-def project_keep(here, mixed, weights, got, masks):
+    )(here, *in_hbm([out_weight]), mixed, *weights)
+
+
+def project_add(here, mixed, weights, got, masks, first, dtype):
     count = mixed.shape[0]
-    half, width = len(masks) // 2, got.shape[2]
-    return pl.pallas_call(
-        lambda *refs: project_keep_kernel(masks, *refs),
-        out_shape=(shape((half, count, width)), shape((half, count, width), jnp.float32)),
+    width = got.shape[2]
+    return pl.pallas_call(
+        lambda *refs: project_add_kernel(masks, first, *refs),
+        out_shape=shape((len(masks), count, width), dtype),
         in_specs=[SMEM, VMEM] + [VMEM] * len(weights) + [VMEM],
-        out_specs=(VMEM, VMEM),
+        out_specs=VMEM,
         compiler_params=params(6),
         cost_estimate=project_cost(mixed, len(masks) * width),
     )(here, mixed, *weights, got)
@@ -514,25 +573,33 @@
 
 def plan(devices, own_width):
     bits = [1 << b for b in range(devices.bit_length() - 1)]
-    half = own_width // 2
+    first = own_width * SHARE // 8
     return [
-        (0, half, bits),
-        (half, half, [bits[0], bits[2], bits[1]] + bits[3:]),
+        (0, first, bits),
+        (first, own_width - first, [bits[0], bits[2], bits[1]] + bits[3:]),
     ]
 
 
-def project_and_scatter(here, devices, x, weights, chunks):
+def project_and_scatter(here, devices, x, out_weight, weights, chunks, last):
     masks = [fold_masks(order) for _, _, order in chunks]
-    half = devices // 2
-    state, got = [], []
-    for at, (start, width, order) in enumerate(chunks):
-        out = project_send(here, x, weights[at], masks[at][half:], width)
+    half, quarter = devices // 2, devices // 4
+    got, sends, keeps = [], [], []
+    weights = [list(w) for w in weights]
+    for at, (_, width, order) in enumerate(chunks):
+        out, *more = project_send(
+            here, x, weights[at], masks[at][half:], width, out_weight, last[at], devices
+        )
+        if more:
+            weights[at + 1] += more
         got.append(swap(out, order[0], devices))
         x = after(x, out)
-    for at, (start, _, _) in enumerate(chunks):
-        send, keep = project_keep(here, x, weights[at], got[at], masks[at][:half])
-        state.append((send, keep))
-        x = after(x, send)
+    for dtype, into, first in ((jnp.bfloat16, sends, quarter), (jnp.float32, keeps, 0)):
+        for at, w in enumerate(weights):
+            part = masks[at][first : first + quarter]
+            y = project_add(here, x, w, got[at], part, first, dtype)
+            into.append(y)
+            x = after(x, y)
+    state = list(zip(sends, keeps))
     stages = len(chunks[0][2])
     for stage in range(1, stages):
         arrived = [swap(send, chunks[at][2][stage], devices) for at, (send, _) in enumerate(state)]
@@ -557,32 +624,49 @@
     here = lax.axis_index("ctx").astype(jnp.int32)[None]
     source, lengths, offsets = page_source[None], page_lengths[None], page_offsets[None]
     positions = query_positions[None]
-    pieces = prepare_rows(
-        here, pool_keys, pool_values, key_scales, value_scales, source, lengths, offsets
-    )
+    depth = out_weight.shape[0]
+    chunks = plan(devices, out_weight.shape[1] // devices)
+    first_part, send_part = [], []
+    attention_part, side_part = [
+        [(0, depth, start, width)] for start, width, _ in chunks
+    ]
+    prepared = prepare_rows(
+        here,
+        out_weight,
+        first_part,
+        devices,
+        pool_keys,
+        pool_values,
+        key_scales,
+        value_scales,
+        source,
+        lengths,
+        offsets,
+    )
+    pieces, first_weights = prepared[:KV], prepared[KV:]
     far = range(KV // 2, KV)
     arrived = [pieces[0]] + [swap(pieces[k], 2 * k, devices) for k in range(1, KV)]
-    depth = out_weight.shape[0]
-    chunks = plan(devices, out_weight.shape[1] // devices)
-    (start, width, _), (later, later_width, _) = chunks
-    early_rows = depth * EARLY // 16
-    early = [(0, early_rows, later, later_width)]
-    late = [(0, depth, start, width)]
-    if early_rows < depth:
-        late.append((early_rows, depth, later, later_width))
-    turned, key_positions, *early_weights = side(
-        here, source, lengths, offsets, positions, queries, out_weight, early, devices
+    turned, key_positions, *side_weights = side(
+        here, source, lengths, offsets, positions, queries, out_weight, side_part, devices
     )
     near = assemble(arrived[: KV // 2])
     far = assemble(arrived[KV // 2 :])
     context = [near, far, swap(near, 1, devices), swap(far, 1, devices)]
-    leaving = order_pages(here, page_source, context)
-    pages = [leaving[0]] + [swap(leaving[k], 2 * k, devices) for k in range(1, KV)]
+    near_pages, far_pages = order_pages(here, page_source, context)
+    held, heads = send_pages(near_pages, far_pages, devices)
     mixed, *late_weights = attend(
-        context, turned, key_positions, positions, out_weight, late, devices
-    )
-    output = project_and_scatter(here, devices, mixed, [late_weights[:1], early_weights + late_weights[1:]], chunks)
-    mine, partner = collect_heads(here, pages)
+        context, turned, key_positions, positions, out_weight, attention_part, devices
+    )
+    output = project_and_scatter(
+        here,
+        devices,
+        mixed,
+        out_weight,
+        [[*first_weights, *late_weights], side_weights],
+        chunks,
+        [send_part, []],
+    )
+    mine, partner = collect_heads(here, held, heads)
     new_keys, new_values = settle(here, mine, swap(partner, 1, devices))
     return (new_keys, new_values, output)
 

time: 89.7 us -> 94.6 us (1.055)
  waiting for transfers between devices: 31.9 us -> 45.4 us
  starting transfers between devices: 34 us -> 24.6 us
    ppermute x25 -> x21, waiting for transfers between devices: 31.9 us -> 45.4 us  [swap(): return lax.ppermute(x, 'ctx', [(d, d ^ bits) for d in range(devices)])]
    ppermute x25 -> x21, starting transfers between devices: 34 us -> 24.6 us  [swap(): return lax.ppermute(x, 'ctx', [(d, d ^ bits) for d in range(devices)])]
    pallas_call x1, Pallas kernels: 7.37 us -> 6.06 us  [attend(): pl.pallas_call(lambda *refs: attention_kernel(pieces, owners, *refs), out...]
    pallas_call x1, Pallas kernels: 5.5 us -> 6.72 us  [side(): pl.pallas_call(lambda *refs: side_kernel(pieces, owners, *refs), out_shap...]
    pallas_call x7 -> x11, Pallas kernels: 7.91 us -> 8.79 us  [the longest x4 3.06 us: project_add(): pl.pallas_call(lambda *refs: project_add_kernel(masks, first, *refs), out...]
  transfers between devices with their start and end apart: 25 -> 21, of which waited for: 11 -> 9; matrix products, arithmetic and copies ran while one was open for 0% -> 0% of each run, Pallas kernels for 12% -> 14%
where the time goes in v3:
time: 94.6 us; the launch traced here: 94.4 us
  waiting for transfers between devices  45.4 us (48%)
  starting transfers between devices  24.6 us (26%)
  Pallas kernels  23.5 us (25%)
    ppermute x21, waiting for transfers between devices, swap(): return lax.ppermute(x, 'ctx', [(d, d ^ bits) for d in range(devices)])  45.4 us
    ppermute x21, starting transfers between devices, swap(): return lax.ppermute(x, 'ctx', [(d, d ^ bits) for d in range(devices)])  24.6 us
    pallas_call x1, Pallas kernels, side(): pl.pallas_call(lambda *refs: side_kernel(pieces, owners, *refs), out_shap...  6.72 us
    pallas_call x1, Pallas kernels, attend(): pl.pallas_call(lambda *refs: attention_kernel(pieces, owners, *refs), out...  6.06 us
    pallas_call x4, Pallas kernels, project_add(): pl.pallas_call(lambda *refs: project_add_kernel(masks, first, *refs), out...  3.06 us
    pallas_call x2, Pallas kernels, project_send(): pl.pallas_call(lambda *refs: project_send_kernel(masks, pieces, owners, *...  2.85 us
  transfers between devices with their start and end apart: 21, of which 9 were waited for; matrix products, arithmetic and copies ran while one was open for 0% of the time, Pallas kernels for 14%

profile of v3, /device:TPU:0, one launch (start us, length us, event | category | flops | bytes accessed | tf_op | source)
XLA Modules:
  0.0 94.4 jit_solution(12031104812962203839)
XLA Ops:
  0.6 1.9 %prepare_rows.1 = (bf16[2,128,128]{2,1,0:T(8,128)(2,1)S(1)}, bf16[2,128,128]{2,1,0:T(8,128)(2,1)S(1)}, bf16[2,128,128]{2,1,0:T(8,128)(2,1)S(1)}, bf16[2,128,128]...) custom-call(s32[1]{0:T(128)} %bitcast.refs_0_.here_ref, ...), custom_call_target="tpu_custom_call" | custom-call | flops 2621440 | bytes 1048576 | tf_op jit(solution)/shard_map/prepare_rows/pallas_call | solution.py:145
  2.5 4.1 %collective-permute-start.3 = (bf16[2,128,128]{2,1,0:T(8,128)(2,1)S(1)}, bf16[2,128,128]{2,1,0:T(8,128)(2,1)S(1)}, u32[]{:S(2)}, u32[]{:S(2)}) collective-permute-start(bf16[2,128,128]{2,1,0:T(8,128)(2,1)S(1)} %get-tuple-element.39), channel_id=1, source_target_pairs={{0,8},{1,9},{2,10},{3,11},{4,12},{5,13},{6,14},{7,15},{8,0},{9,1},... | collective-permute-start | bytes 196616 | tf_op jit(solution)/shard_map/ppermute | solution.py:567
  6.6 1.3 %collective-permute-start.4 = (bf16[2,128,128]{2,1,0:T(8,128)(2,1)S(1)}, bf16[2,128,128]{2,1,0:T(8,128)(2,1)S(1)}, u32[]{:S(2)}, u32[]{:S(2)}) collective-permute-start(bf16[2,128,128]{2,1,0:T(8,128)(2,1)S(1)} %get-tuple-element.40), channel_id=1, source_target_pairs={{0,10},{1,11},{2,8},{3,9},{4,14},{5,15},{6,12},{7,13},{8,2},{9,3},... | collective-permute-start | bytes 196616 | tf_op jit(solution)/shard_map/ppermute | solution.py:567
  8.2 3.9 %collective-permute-start.5 = (bf16[2,128,128]{2,1,0:T(8,128)(2,1)S(1)}, bf16[2,128,128]{2,1,0:T(8,128)(2,1)S(1)}, u32[]{:S(2)}, u32[]{:S(2)}) collective-permute-start(bf16[2,128,128]{2,1,0:T(8,128)(2,1)S(1)} %get-tuple-element.41), channel_id=1, source_target_pairs={{0,12},{1,13},{2,14},{3,15},{4,8},{5,9},{6,10},{7,11},{8,4},{9,5},... | collective-permute-start | bytes 196616 | tf_op jit(solution)/shard_map/ppermute | solution.py:567
  12.0 1.2 %collective-permute-start.6 = (bf16[2,128,128]{2,1,0:T(8,128)(2,1)S(1)}, bf16[2,128,128]{2,1,0:T(8,128)(2,1)S(1)}, u32[]{:S(2)}, u32[]{:S(2)}) collective-permute-start(bf16[2,128,128]{2,1,0:T(8,128)(2,1)S(1)} %get-tuple-element.42), channel_id=1, source_target_pairs={{0,14},{1,15},{2,12},{3,13},{4,10},{5,11},{6,8},{7,9},{8,6},{9,7},... | collective-permute-start | bytes 196616 | tf_op jit(solution)/shard_map/ppermute | solution.py:567
  13.2 2.7 %collective-permute-done.4.refs_1_ = bf16[2,128,128]{2,1,0:T(8,128)(2,1)S(1)} collective-permute-done((bf16[2,128,128]{2,1,0:T(8,128)(2,1)S(1)}, bf16[2,128,128]{2,1,0:T(8,128)(2,1)S(1)}, u32[]{:S(2)}, u32[]{:S(2)}) %collective-permute-start.4) | collective-permute-done | bytes 65568 | tf_op jit(solution)/shard_map/ppermute | solution.py:567
  15.9 1.5 %collective-permute-start.2 = (bf16[2,128,128]{2,1,0:T(8,128)(2,1)S(1)}, bf16[2,128,128]{2,1,0:T(8,128)(2,1)S(1)}, u32[]{:S(2)}, u32[]{:S(2)}) collective-permute-start(bf16[2,128,128]{2,1,0:T(8,128)(2,1)S(1)} %get-tuple-element.38), channel_id=1, source_target_pairs={{0,6},{1,7},{2,4},{3,5},{4,2},{5,3},{6,0},{7,1},{8,14},{9,15},{10,... | collective-permute-start | bytes 196616 | tf_op jit(solution)/shard_map/ppermute | solution.py:567
  17.5 1.7 %collective-permute-done.6.refs_3_ = bf16[2,128,128]{2,1,0:T(8,128)(2,1)S(1)} collective-permute-done((bf16[2,128,128]{2,1,0:T(8,128)(2,1)S(1)}, bf16[2,128,128]{2,1,0:T(8,128)(2,1)S(1)}, u32[]{:S(2)}, u32[]{:S(2)}) %collective-permute-start.6) | collective-permute-done | bytes 65568 | tf_op jit(solution)/shard_map/ppermute | solution.py:567
  19.2 1.9 %collective-permute-done.2.refs_3_ = bf16[2,128,128]{2,1,0:T(8,128)(2,1)S(1)} collective-permute-done((bf16[2,128,128]{2,1,0:T(8,128)(2,1)S(1)}, bf16[2,128,128]{2,1,0:T(8,128)(2,1)S(1)}, u32[]{:S(2)}, u32[]{:S(2)}) %collective-permute-start.2) | collective-permute-done | bytes 65568 | tf_op jit(solution)/shard_map/ppermute | solution.py:567
  21.2 6.7 %side.1 = (bf16[1024,128]{1,0:T(8,128)(2,1)S(1)}, f32[1,2048]{1,0:T(1,128)S(1)}, bf16[1024,8192]{1,0:T(8,128)(2,1)S(1)}) custom-call(s32[1]{0:T(128)} %bitcast.refs_0_.here_ref, bf16[1024,16384]{1,0:T(8,128)(2,1)} %refs_1_.7, f32[2,128]{1,0:T(2,128)} %constant.6.clone.refs_4_.refs_2_, s32[1,128]{1,0:T(1,128)} %bitcast.11, s32[1,128]{1,0:T(1,128)} %bitcast.16, ...), custom_call_target="tpu_custom_call" | custom-call | flops 1048576 | bytes 67108864 | tf_op jit(solution)/shard_map/side/pallas_call | solution.py:216
  28.0 6.1 %attend.1 = (bf16[128,1024]{1,0:T(8,128)(2,1)S(1)}, bf16[1024,8192]{1,0:T(8,128)(2,1)S(1)}) custom-call(bf16[1024,16384]{1,0:T(8,128)(2,1)} %refs_1_.7, bf16[4,2,128,128]{3,2,1,0:T(8,128)(2,1)S(1)} %shard_map.139.refs_0_.refs_1_, bf16[4,2,128,128]{3,2,1,0:T(8,128)(2,1)S(1)} %shard_map.140.refs_1_.refs_2_, ...), custom_call_target="tpu_custom_call" | custom-call | flops 1073741824 | bytes 1048576 | tf_op jit(solution)/shard_map/attend/pallas_call | solution.py:429
  34.0 1.4 %shard_map.143 = bf16[8,128,512]{2,1,0:T(8,128)(2,1)S(1)} custom-call(s32[1]{0:T(128)} %bitcast.refs_0_.here_ref, bf16[1024,16384]{1,0:T(8,128)(2,1)} %refs_1_.7, bf16[128,1024]{1,0:T(8,128)(2,1)S(1)} %get-tuple-element.62.refs_2_.refs_1_, bf16[1024,8192]{1,0:T(8,128)(2,1)S(1)} %get-tuple-element.52.refs_3_.refs_2_), custom_call_target="tpu_custom_call" | custom-call | flops 1073741824 | bytes 8388608 | tf_op jit(solution)/shard_map/pallas_call | solution.py:495
  36.1 1.4 %shard_map.144 = bf16[8,128,512]{2,1,0:T(8,128)(2,1)S(1)} custom-call(s32[1]{0:T(128)} %bitcast.refs_0_.here_ref, bf16[1024,16384]{1,0:T(8,128)(2,1)} %refs_1_.7, bf16[128,1024]{1,0:T(8,128)(2,1)S(1)} %get-tuple-element.62.refs_2_.refs_1_, bf16[1024,8192]{1,0:T(8,128)(2,1)S(1)} %get-tuple-element.54.refs_3_.refs_2_), custom_call_target="tpu_custom_call" | custom-call | flops 1073741824 | bytes 8388608 | tf_op jit(solution)/shard_map/pallas_call | solution.py:495
  37.6 0.9 order_pages.1
  38.5 2.3 %collective-permute-start.9 = (bf16[1,4,16,16,128]{4,3,2,1,0:T(8,128)(2,1)S(1)}, bf16[1,4,16,16,128]{4,3,2,1,0:T(8,128)(2,1)S(1)}, u32[]{:S(2)}, u32[]{:S(2)}) collective-permute-start(bf16[1,4,16,16,128]{4,3,2,1,0:T(8,128)(2,1)S(1)} %bitcast.14), channel_id=1, source_target_pairs={{0,8},{1,9},{2,10},{3,11},{4,12},{5,13},{6,14},{7,15},{8,0},{9,1},... | collective-permute-start | bytes 786440 | tf_op jit(solution)/shard_map/ppermute | solution.py:567
  40.8 0.8 shard_map.145
  41.6 0.8 shard_map.146
  42.3 2.8 %collective-permute-start.18 = (bf16[4,128,512]{2,1,0:T(8,128)(2,1)S(1)}, bf16[4,128,512]{2,1,0:T(8,128)(2,1)S(1)}, u32[]{:S(2)}, u32[]{:S(2)}) collective-permute-start(bf16[4,128,512]{2,1,0:T(8,128)(2,1)S(1)} %shard_map.146), channel_id=1, source_target_pairs={{0,4},{1,5},{2,6},{3,7},{4,0},{5,1},{6,2},{7,3},{8,12},{9,13},{10,... | collective-permute-start | bytes 1572872 | tf_op jit(solution)/shard_map/ppermute | solution.py:567
  45.2 0.7 collective-permute-start.15
  45.9 7.9 %collective-permute-done.9.refs_1_.refs_2_ = bf16[1,4,16,16,128]{4,3,2,1,0:T(8,128)(2,1)S(1)} collective-permute-done((bf16[1,4,16,16,128]{4,3,2,1,0:T(8,128)(2,1)S(1)}, bf16[1,4,16,16,128]{4,3,2,1,0:T(8,128)(2,1)S(1)}, u32[]{:S(2)}, u32[]{:S(2)}) %collective-permute-start.9) | collective-permute-done | bytes 262176 | tf_op jit(solution)/shard_map/ppermute | solution.py:567
  54.2 12.5 %collective-permute-done.10.refs_2_.refs_3_ = bf16[2,2,16,16,128]{4,3,2,1,0:T(8,128)(2,1)S(1)} collective-permute-done((bf16[2,2,16,16,128]{4,3,2,1,0:T(8,128)(2,1)S(1)}, bf16[2,2,16,16,128]{4,3,2,1,0:T(8,128)(2,1)S(1)}, u32[]{:S(2)}, u32[]{:S(2)}) %collective-permute-start.10) | collective-permute-done | bytes 262176 | tf_op jit(solution)/shard_map/ppermute | solution.py:567
  66.7 1.6 %collective-permute-start.11 = (bf16[4,1,16,16,128]{4,3,2,1,0:T(8,128)(2,1)S(1)}, bf16[4,1,16,16,128]{4,3,2,1,0:T(8,128)(2,1)S(1)}, u32[]{:S(2)}, u32[]{:S(2)}) collective-permute-start(bf16[4,1,16,16,128]{4,3,2,1,0:T(8,128)(2,1)S(1)} %shard_map.142), channel_id=1, source_target_pairs={{0,2},{1,3},{2,0},{3,1},{4,6},{5,7},{6,4},{7,5},{8,10},{9,11},{10,... | collective-permute-start | bytes 786440 | tf_op jit(solution)/shard_map/ppermute | solution.py:567
  68.3 0.8 shard_map.147.keep_ref
  69.0 0.8 shard_map.150.keep_ref
  70.7 5.2 %collective-permute-done.11.refs_4_ = bf16[4,1,16,16,128]{4,3,2,1,0:T(8,128)(2,1)S(1)} collective-permute-done((bf16[4,1,16,16,128]{4,3,2,1,0:T(8,128)(2,1)S(1)}, bf16[4,1,16,16,128]{4,3,2,1,0:T(8,128)(2,1)S(1)}, u32[]{:S(2)}, u32[]{:S(2)}) %collective-permute-start.11) | collective-permute-done | bytes 262176 | tf_op jit(solution)/shard_map/ppermute | solution.py:567
  76.2 3.9 %collective-permute-done.19.got_ref = bf16[2,128,512]{2,1,0:T(8,128)(2,1)S(1)} collective-permute-done((bf16[2,128,512]{2,1,0:T(8,128)(2,1)S(1)}, bf16[2,128,512]{2,1,0:T(8,128)(2,1)S(1)}, u32[]{:S(2)}, u32[]{:S(2)}) %collective-permute-start.19) | collective-permute-done | bytes 262176 | tf_op jit(solution)/shard_map/ppermute | solution.py:567
  80.2 1.7 %collective-permute-start.20 = (bf16[1,128,512]{2,1,0:T(8,128)(2,1)S(1)}, bf16[1,128,512]{2,1,0:T(8,128)(2,1)S(1)}, u32[]{:S(2)}, u32[]{:S(2)}) collective-permute-start(bf16[1,128,512]{2,1,0:T(8,128)(2,1)S(1)} %get-tuple-element.66), channel_id=1, source_target_pairs={{0,8},{1,9},{2,10},{3,11},{4,12},{5,13},{6,14},{7,15},{8,0},{9,1},... | collective-permute-start | bytes 393224 | tf_op jit(solution)/shard_map/ppermute | solution.py:567
  81.9 1.4 %collective-permute-start.17 = (bf16[1,128,512]{2,1,0:T(8,128)(2,1)S(1)}, bf16[1,128,512]{2,1,0:T(8,128)(2,1)S(1)}, u32[]{:S(2)}, u32[]{:S(2)}) collective-permute-start(bf16[1,128,512]{2,1,0:T(8,128)(2,1)S(1)} %get-tuple-element.61), channel_id=1, source_target_pairs={{0,8},{1,9},{2,10},{3,11},{4,12},{5,13},{6,14},{7,15},{8,0},{9,1},... | collective-permute-start | bytes 393224 | tf_op jit(solution)/shard_map/ppermute | solution.py:567
  83.3 0.8 settle.1
  84.1 7.6 %collective-permute-done.20.refs_3_ = bf16[1,128,512]{2,1,0:T(8,128)(2,1)S(1)} collective-permute-done((bf16[1,128,512]{2,1,0:T(8,128)(2,1)S(1)}, bf16[1,128,512]{2,1,0:T(8,128)(2,1)S(1)}, u32[]{:S(2)}, u32[]{:S(2)}) %collective-permute-start.20) | collective-permute-done | bytes 131104 | tf_op jit(solution)/shard_map/ppermute | solution.py:567
  91.7 1.9 %collective-permute-done.17.refs_1_ = bf16[1,128,512]{2,1,0:T(8,128)(2,1)S(1)} collective-permute-done((bf16[1,128,512]{2,1,0:T(8,128)(2,1)S(1)}, bf16[1,128,512]{2,1,0:T(8,128)(2,1)S(1)}, u32[]{:S(2)}, u32[]{:S(2)}) %collective-permute-start.17) | collective-permute-done | bytes 131104 | tf_op jit(solution)/shard_map/ppermute | solution.py:567
  93.6 0.8 finish.1
  (35 shorter events, 2.7 us)
Async XLA Ops:
  2.5 10.7 %collective-permute-start.3 = (bf16[2,128,128]{2,1,0:T(8,128)(2,1)S(1)}, bf16[2,128,128]{2,1,0:T(8,128)(2,1)S(1)}, u32[]{:S(2)}, u32[]{:S(2)}) collective-permute-start(bf16[2,128,128]{2,1,0:T(8,128)(2,1)S(1)} %get-tuple-element.39), channel_id=1, source_target_pairs={{0,8},{1,9},{2,10},{3,11},{4,12},{5,13},{6,14},{7,15},{8,0},{9,1},... | collective-permute-start | bytes 196616 | tf_op jit(solution)/shard_map/ppermute | solution.py:567
  6.6 9.3 %collective-permute-start.4 = (bf16[2,128,128]{2,1,0:T(8,128)(2,1)S(1)}, bf16[2,128,128]{2,1,0:T(8,128)(2,1)S(1)}, u32[]{:S(2)}, u32[]{:S(2)}) collective-permute-start(bf16[2,128,128]{2,1,0:T(8,128)(2,1)S(1)} %get-tuple-element.40), channel_id=1, source_target_pairs={{0,10},{1,11},{2,8},{3,9},{4,14},{5,15},{6,12},{7,13},{8,2},{9,3},... | collective-permute-start | bytes 196616 | tf_op jit(solution)/shard_map/ppermute | solution.py:567
  7.9 11.3 %collective-permute-start = (bf16[2,128,128]{2,1,0:T(8,128)(2,1)S(1)}, bf16[2,128,128]{2,1,0:T(8,128)(2,1)S(1)}, u32[]{:S(2)}, u32[]{:S(2)}) collective-permute-start(bf16[2,128,128]{2,1,0:T(8,128)(2,1)S(1)} %get-tuple-element.36), channel_id=1, source_target_pairs={{0,2},{1,3},{2,0},{3,1},{4,6},{5,7},{6,4},{7,5},{8,10},{9,11},{10,... | collective-permute-start | bytes 196616 | tf_op jit(solution)/shard_map/ppermute | solution.py:567
  8.2 9.3 %collective-permute-start.5 = (bf16[2,128,128]{2,1,0:T(8,128)(2,1)S(1)}, bf16[2,128,128]{2,1,0:T(8,128)(2,1)S(1)}, u32[]{:S(2)}, u32[]{:S(2)}) collective-permute-start(bf16[2,128,128]{2,1,0:T(8,128)(2,1)S(1)} %get-tuple-element.41), channel_id=1, source_target_pairs={{0,12},{1,13},{2,14},{3,15},{4,8},{5,9},{6,10},{7,11},{8,4},{9,5},... | collective-permute-start | bytes 196616 | tf_op jit(solution)/shard_map/ppermute | solution.py:567
  12.0 7.1 %collective-permute-start.6 = (bf16[2,128,128]{2,1,0:T(8,128)(2,1)S(1)}, bf16[2,128,128]{2,1,0:T(8,128)(2,1)S(1)}, u32[]{:S(2)}, u32[]{:S(2)}) collective-permute-start(bf16[2,128,128]{2,1,0:T(8,128)(2,1)S(1)} %get-tuple-element.42), channel_id=1, source_target_pairs={{0,14},{1,15},{2,12},{3,13},{4,10},{5,11},{6,8},{7,9},{8,6},{9,7},... | collective-permute-start | bytes 196616 | tf_op jit(solution)/shard_map/ppermute | solution.py:567
  13.2 6.0 %collective-permute-start.1 = (bf16[2,128,128]{2,1,0:T(8,128)(2,1)S(1)}, bf16[2,128,128]{2,1,0:T(8,128)(2,1)S(1)}, u32[]{:S(2)}, u32[]{:S(2)}) collective-permute-start(bf16[2,128,128]{2,1,0:T(8,128)(2,1)S(1)} %get-tuple-element.37), channel_id=1, source_target_pairs={{0,4},{1,5},{2,6},{3,7},{4,0},{5,1},{6,2},{7,3},{8,12},{9,13},{10,... | collective-permute-start | bytes 196616 | tf_op jit(solution)/shard_map/ppermute | solution.py:567
  15.9 5.2 %collective-permute-start.2 = (bf16[2,128,128]{2,1,0:T(8,128)(2,1)S(1)}, bf16[2,128,128]{2,1,0:T(8,128)(2,1)S(1)}, u32[]{:S(2)}, u32[]{:S(2)}) collective-permute-start(bf16[2,128,128]{2,1,0:T(8,128)(2,1)S(1)} %get-tuple-element.38), channel_id=1, source_target_pairs={{0,6},{1,7},{2,4},{3,5},{4,2},{5,3},{6,0},{7,1},{8,14},{9,15},{10,... | collective-permute-start | bytes 196616 | tf_op jit(solution)/shard_map/ppermute | solution.py:567
  19.1 8.8 %collective-permute-start.8 = (bf16[4,2,128,128]{3,2,1,0:T(8,128)(2,1)S(1)}, bf16[4,2,128,128]{3,2,1,0:T(8,128)(2,1)S(1)}, u32[]{:S(2)}, u32[]{:S(2)}) collective-permute-start(bf16[4,2,128,128]{3,2,1,0:T(8,128)(2,1)S(1)} %shard_map.140.refs_1_.refs_2_), channel_id=1, source_target_pairs={{0,1},{1,0},{2,3},{3,2},{4,5},{5,4},{6,7},{7,6},{8,9},{9,8},{10,11... | collective-permute-start | bytes 786440 | tf_op jit(solution)/shard_map/ppermute | solution.py:567
  21.1 6.8 %collective-permute-start.7 = (bf16[4,2,128,128]{3,2,1,0:T(8,128)(2,1)S(1)}, bf16[4,2,128,128]{3,2,1,0:T(8,128)(2,1)S(1)}, u32[]{:S(2)}, u32[]{:S(2)}) collective-permute-start(bf16[4,2,128,128]{3,2,1,0:T(8,128)(2,1)S(1)} %shard_map.139.refs_0_.refs_1_), channel_id=1, source_target_pairs={{0,1},{1,0},{2,3},{3,2},{4,5},{5,4},{6,7},{7,6},{8,9},{9,8},{10,11... | collective-permute-start | bytes 786440 | tf_op jit(solution)/shard_map/ppermute | solution.py:567
  21.2 6.8 %copy-start.1 = (s32[128]{0:T(128)S(1)}, s32[128]{0:T(128)}, u32[]{:S(2)}) copy-start(s32[128]{0:T(128)} %param.19) | copy-start | bytes 1540
  35.5 5.3 %collective-permute-start.13 = (bf16[8,128,512]{2,1,0:T(8,128)(2,1)S(1)}, bf16[8,128,512]{2,1,0:T(8,128)(2,1)S(1)}, u32[]{:S(2)}, u32[]{:S(2)}) collective-permute-start(bf16[8,128,512]{2,1,0:T(8,128)(2,1)S(1)} %shard_map.143), channel_id=1, source_target_pairs={{0,1},{1,0},{2,3},{3,2},{4,5},{5,4},{6,7},{7,6},{8,9},{9,8},{10,11... | collective-permute-start | bytes 3145736 | tf_op jit(solution)/shard_map/ppermute | solution.py:567
  36.1 1.6 %copy-start = (s32[128]{0:T(128)S(1)}, s32[128]{0:T(128)}, u32[]{:S(2)}) copy-start(s32[128]{0:T(128)} %source_ref.1) | copy-start | bytes 1540
  37.5 4.1 %collective-permute-start.14 = (bf16[8,128,512]{2,1,0:T(8,128)(2,1)S(1)}, bf16[8,128,512]{2,1,0:T(8,128)(2,1)S(1)}, u32[]{:S(2)}, u32[]{:S(2)}) collective-permute-start(bf16[8,128,512]{2,1,0:T(8,128)(2,1)S(1)} %shard_map.144), channel_id=1, source_target_pairs={{0,1},{1,0},{2,3},{3,2},{4,5},{5,4},{6,7},{7,6},{8,9},{9,8},{10,11... | collective-permute-start | bytes 3145736 | tf_op jit(solution)/shard_map/ppermute | solution.py:567
  38.5 15.3 %collective-permute-start.9 = (bf16[1,4,16,16,128]{4,3,2,1,0:T(8,128)(2,1)S(1)}, bf16[1,4,16,16,128]{4,3,2,1,0:T(8,128)(2,1)S(1)}, u32[]{:S(2)}, u32[]{:S(2)}) collective-permute-start(bf16[1,4,16,16,128]{4,3,2,1,0:T(8,128)(2,1)S(1)} %bitcast.14), channel_id=1, source_target_pairs={{0,8},{1,9},{2,10},{3,11},{4,12},{5,13},{6,14},{7,15},{8,0},{9,1},... | collective-permute-start | bytes 786440 | tf_op jit(solution)/shard_map/ppermute | solution.py:567
  42.3 27.5 %collective-permute-start.18 = (bf16[4,128,512]{2,1,0:T(8,128)(2,1)S(1)}, bf16[4,128,512]{2,1,0:T(8,128)(2,1)S(1)}, u32[]{:S(2)}, u32[]{:S(2)}) collective-permute-start(bf16[4,128,512]{2,1,0:T(8,128)(2,1)S(1)} %shard_map.146), channel_id=1, source_target_pairs={{0,4},{1,5},{2,6},{3,7},{4,0},{5,1},{6,2},{7,3},{8,12},{9,13},{10,... | collective-permute-start | bytes 1572872 | tf_op jit(solution)/shard_map/ppermute | solution.py:567
  45.2 25.4 %collective-permute-start.15 = (bf16[4,128,512]{2,1,0:T(8,128)(2,1)S(1)}, bf16[4,128,512]{2,1,0:T(8,128)(2,1)S(1)}, u32[]{:S(2)}, u32[]{:S(2)}) collective-permute-start(bf16[4,128,512]{2,1,0:T(8,128)(2,1)S(1)} %shard_map.145), channel_id=1, source_target_pairs={{0,2},{1,3},{2,0},{3,1},{4,6},{5,7},{6,4},{7,5},{8,10},{9,11},{10,... | collective-permute-start | bytes 1572872 | tf_op jit(solution)/shard_map/ppermute | solution.py:567
  53.9 12.8 %collective-permute-start.10 = (bf16[2,2,16,16,128]{4,3,2,1,0:T(8,128)(2,1)S(1)}, bf16[2,2,16,16,128]{4,3,2,1,0:T(8,128)(2,1)S(1)}, u32[]{:S(2)}, u32[]{:S(2)}) collective-permute-start(bf16[2,2,16,16,128]{4,3,2,1,0:T(8,128)(2,1)S(1)} %shard_map.141), channel_id=1, source_target_pairs={{0,4},{1,5},{2,6},{3,7},{4,0},{5,1},{6,2},{7,3},{8,12},{9,13},{10,... | collective-permute-start | bytes 786440 | tf_op jit(solution)/shard_map/ppermute | solution.py:567
  66.7 9.2 %collective-permute-start.11 = (bf16[4,1,16,16,128]{4,3,2,1,0:T(8,128)(2,1)S(1)}, bf16[4,1,16,16,128]{4,3,2,1,0:T(8,128)(2,1)S(1)}, u32[]{:S(2)}, u32[]{:S(2)}) collective-permute-start(bf16[4,1,16,16,128]{4,3,2,1,0:T(8,128)(2,1)S(1)} %shard_map.142), channel_id=1, source_target_pairs={{0,2},{1,3},{2,0},{3,1},{4,6},{5,7},{6,4},{7,5},{8,10},{9,11},{10,... | collective-permute-start | bytes 786440 | tf_op jit(solution)/shard_map/ppermute | solution.py:567
  69.9 10.2 %collective-permute-start.19 = (bf16[2,128,512]{2,1,0:T(8,128)(2,1)S(1)}, bf16[2,128,512]{2,1,0:T(8,128)(2,1)S(1)}, u32[]{:S(2)}, u32[]{:S(2)}) collective-permute-start(bf16[2,128,512]{2,1,0:T(8,128)(2,1)S(1)} %get-tuple-element.64), channel_id=1, source_target_pairs={{0,2},{1,3},{2,0},{3,1},{4,6},{5,7},{6,4},{7,5},{8,10},{9,11},{10,... | collective-permute-start | bytes 786440 | tf_op jit(solution)/shard_map/ppermute | solution.py:567
  70.6 11.2 %collective-permute-start.16 = (bf16[2,128,512]{2,1,0:T(8,128)(2,1)S(1)}, bf16[2,128,512]{2,1,0:T(8,128)(2,1)S(1)}, u32[]{:S(2)}, u32[]{:S(2)}) collective-permute-start(bf16[2,128,512]{2,1,0:T(8,128)(2,1)S(1)} %get-tuple-element.59), channel_id=1, source_target_pairs={{0,4},{1,5},{2,6},{3,7},{4,0},{5,1},{6,2},{7,3},{8,12},{9,13},{10,... | collective-permute-start | bytes 786440 | tf_op jit(solution)/shard_map/ppermute | solution.py:567
  76.1 7.2 %collective-permute-start.12 = (bf16[128,1024]{1,0:T(8,128)(2,1)S(1)}, bf16[128,1024]{1,0:T(8,128)(2,1)S(1)}, u32[]{:S(2)}, u32[]{:S(2)}) collective-permute-start(bf16[128,1024]{1,0:T(8,128)(2,1)S(1)} %get-tuple-element.46), channel_id=1, source_target_pairs={{0,1},{1,0},{2,3},{3,2},{4,5},{5,4},{6,7},{7,6},{8,9},{9,8},{10,11... | collective-permute-start | bytes 786440 | tf_op jit(solution)/shard_map/ppermute | solution.py:567
  80.2 11.5 %collective-permute-start.20 = (bf16[1,128,512]{2,1,0:T(8,128)(2,1)S(1)}, bf16[1,128,512]{2,1,0:T(8,128)(2,1)S(1)}, u32[]{:S(2)}, u32[]{:S(2)}) collective-permute-start(bf16[1,128,512]{2,1,0:T(8,128)(2,1)S(1)} %get-tuple-element.66), channel_id=1, source_target_pairs={{0,8},{1,9},{2,10},{3,11},{4,12},{5,13},{6,14},{7,15},{8,0},{9,1},... | collective-permute-start | bytes 393224 | tf_op jit(solution)/shard_map/ppermute | solution.py:567
  81.9 11.7 %collective-permute-start.17 = (bf16[1,128,512]{2,1,0:T(8,128)(2,1)S(1)}, bf16[1,128,512]{2,1,0:T(8,128)(2,1)S(1)}, u32[]{:S(2)}, u32[]{:S(2)}) collective-permute-start(bf16[1,128,512]{2,1,0:T(8,128)(2,1)S(1)} %get-tuple-element.61), channel_id=1, source_target_pairs={{0,8},{1,9},{2,10},{3,11},{4,12},{5,13},{6,14},{7,15},{8,0},{9,1},... | collective-permute-start | bytes 393224 | tf_op jit(solution)/shard_map/ppermute | solution.py:567
